TPU v7x, 128 devices: a whole 4x4x4 slice. The times are simulated.
128 devices in a mesh: pos: 32 (over x, z, core), tile: 4 (over y).
Axes of the slice: x: 4, y: 4, z: 4, core: 2. Of those that a mesh axis runs over, the one named last changes fastest.
Arguments:
- object_field: float32 [2, 2048, 16384], P(None, 'tile', 'pos'), may hold values from -6 to 6
- probe: float32 [2, 256, 256], replicated, may hold values from -45 to 45
- amplitudes: bfloat16 [4, 32, 32, 256, 256], P('tile', 'pos'), may hold values from 0.099609375 to 3
- corner_rows: int32 [4, 32, 32], P('tile', 'pos'), may hold values from 0 to 511, as said below
- corner_cols: int32 [4, 32, 32], P('tile', 'pos'), may hold values from 0 to 511, as said below
- counts: int32 [4, 32], P('tile', 'pos'), may hold values from 1 to 32, as said below
Outputs:
- object_new: float32 [2, 2048, 16384], P(None, 'tile', 'pos')
- probe_grad: float32 [2, 256, 256], replicated
Inputs may be any that keep to these rules, and one draw needn't show every extreme that they name: Slots from counts[t, p] on are unused. `corner_rows`: counted from the first row of the owner's block. `corner_cols`: counted from the first column of the owner's block.
All inputs are finite; a program needn't handle non-finite values.
Results may differ from a plain program's by a relative error of at most 0.0012.
Values sent between devices are 32-bit elements; how exact they have to be, the bound alone decides.
A program may use at most 64 MiB of HBM per device.

v0:
```python
import functools
import math

import jax
import jax.numpy as jnp
import ml_dtypes
import numpy as np
from jax import lax
from jax.experimental import pallas as pl
from jax.experimental.pallas import tpu as pltpu
from jax.sharding import PartitionSpec as P

N = 256
H = 128
BLOCK = 512
WIDE = 768
LIMIT = 24 * 1024 * 1024


def dft_tables():
    j = np.arange(N)
    angle = (j[:, None] * j[None, :] % N) * (2.0 * np.pi / N)
    re = (np.cos(angle) / np.sqrt(N)).astype(np.float32).astype(ml_dtypes.bfloat16)
    im = (-np.sin(angle) / np.sqrt(N)).astype(np.float32).astype(ml_dtypes.bfloat16)
    return re, im


def stage_tables():
    re, im = dft_tables()

    def pair(a, b, c, d):
        return np.concatenate([np.concatenate([a, b], 1), np.concatenate([c, d], 1)], 0)

    first = [pair(re[:H, q::2], -im[:H, q::2], im[:H, q::2], re[:H, q::2]) for q in (0, 1)]
    second = pair(re, im, -im, re)
    third = [pair(re[q::2, :H], im[q::2, :H], -im[q::2, :H], re[q::2, :H]) for q in (0, 1)]
    fourth = pair(re, -im, im, re)
    return np.stack(first), second, np.stack(third), fourth


def slots_kernel(
    rule, places, first, last,
    rows_ref, cols_ref, count_ref, amp_ref, t1_ref, t2_ref, t3_ref, t4_ref, *refs,
):
    n_pieces = len(places)
    pieces = refs[:n_pieces]
    refs = refs[n_pieces:]
    if first:
        probe_ref = refs[0]
    refs = refs[1 if first else 4 :]
    ext, upd_ref, psum_ref, prb = refs[:4]
    (pat, ext_b, exit_s, near_b, fold_b, back_b, amp_buf, lanes_buf, order, piece_sem, amp_sem) = refs[4:]
    copies = []

    def bring(source, target):
        copies.append(pltpu.make_async_copy(source, target, piece_sem.at[len(copies)]))
        copies[-1].start()

    for piece, (r0, c0) in zip(pieces, places):
        _, h, w = piece.shape
        for b in range(w // H):
            bring(piece.at[:, :, b * H : (b + 1) * H], ext.at[:, c0 // H + b, r0 : r0 + h, :])

    def collect(s, n):
        order[n] = s
        keep = jnp.logical_and(s < count_ref[0, 0], rule(rows_ref[0, 0, s], cols_ref[0, 0, s]))
        return n + keep.astype(jnp.int32)

    total = lax.fori_loop(0, rows_ref.shape[2], collect, jnp.int32(0))

    def amp_copy(i):
        slot = lax.rem(i, 2)
        return pltpu.make_async_copy(amp_ref.at[0, 0, order[i]], amp_buf.at[slot], amp_sem.at[slot])

    @pl.when(total > 0)
    def _():
        amp_copy(0).start()

    if first:
        for b in range(2):
            bring(probe_ref.at[:, :, b * H : (b + 1) * H], lanes_buf.at[:, b])
        upd_ref[...] = jnp.zeros_like(upd_ref)
        psum_ref[...] = jnp.zeros_like(psum_ref)
    for copy in copies:
        copy.wait()
    if first:
        for comp in range(2):
            for q in range(2):
                for b in range(2):
                    prb[comp, q * H : (q + 1) * H, b * H : (b + 1) * H] = lanes_buf[comp, b, pl.ds(q, H, stride=2), :]

    lane = lax.broadcasted_iota(jnp.int32, (H, H), 1)

    def step(i, carry):
        s = order[i]
        r = rows_ref[0, 0, s]
        c = cols_ref[0, 0, s]
        off = lax.rem(c, H)
        c0 = c // H
        back_shift = lax.rem(H - off, H)

        @pl.when(i + 1 < total)
        def _():
            amp_copy(i + 1).start()

        for q in range(2):
            part = []
            for comp in range(2):
                blocks = [
                    pltpu.roll(ext[comp, c0 + b, pl.ds(r + q, H, stride=2), :], back_shift, 1)
                    for b in range(3)
                ]
                part.append(
                    [jnp.where(lane < H - off, blocks[b], blocks[b + 1]) for b in range(2)]
                )
            for b in range(2):
                here = (slice(q * H, (q + 1) * H), slice(b * H, (b + 1) * H))
                pre, pim = prb[0][here], prb[1][here]
                are, aim = part[0][b], part[1][b]
                ere = pre * are - pim * aim
                eim = pre * aim + pim * are
                pat[(0,) + here] = are
                pat[(1,) + here] = aim
                exit_s[(0,) + here] = ere
                exit_s[(1,) + here] = eim
                ext_b[q, 0:H, b * H : (b + 1) * H] = ere.astype(jnp.bfloat16)
                ext_b[q, H:N, b * H : (b + 1) * H] = eim.astype(jnp.bfloat16)

        dot = functools.partial(jnp.dot, preferred_element_type=jnp.float32)
        even = dot(t1_ref[0], ext_b[0])
        odd = dot(t1_ref[1], ext_b[1])
        for comp in range(2):
            e, o = even[comp * H : (comp + 1) * H], odd[comp * H : (comp + 1) * H]
            near_b[0:H, comp * N : (comp + 1) * N] = (e + o).astype(jnp.bfloat16)
            near_b[H:N, comp * N : (comp + 1) * N] = (e - o).astype(jnp.bfloat16)

        amp_copy(i).wait()
        amp = amp_buf.at[lax.rem(i, 2)]
        far = dot(near_b[...], t2_ref[...])
        fre, fim = far[:, :N], far[:, N:]
        ratio = amp[...].astype(jnp.float32) * lax.rsqrt(fre * fre + fim * fim + 0.25)
        for comp, part in enumerate((fre * ratio, fim * ratio)):
            top, low = part[:H], part[H:]
            fold_b[0, comp * H : (comp + 1) * H, :] = (top + low).astype(jnp.bfloat16)
            fold_b[1, comp * H : (comp + 1) * H, :] = (top - low).astype(jnp.bfloat16)

        for q in range(2):
            back = dot(t3_ref[q], fold_b[q])
            for comp in range(2):
                back_b[q * H : (q + 1) * H, comp * N : (comp + 1) * N] = back[comp * H : (comp + 1) * H].astype(
                    jnp.bfloat16
                )
        new = dot(back_b[...], t4_ref[...])
        dre = new[:, :N] - exit_s[0]
        dim = new[:, N:] - exit_s[1]
        psum_ref[0] += pat[0] * dre + pat[1] * dim
        psum_ref[1] += pat[0] * dim - pat[1] * dre
        terms = (prb[0] * dre + prb[1] * dim, prb[0] * dim - prb[1] * dre)
        for comp in range(2):
            for q in range(2):
                z0 = pltpu.roll(terms[comp][q * H : (q + 1) * H, :H], off, 1)
                z1 = pltpu.roll(terms[comp][q * H : (q + 1) * H, H:], off, 1)
                zero = jnp.zeros_like(z0)
                for b, val in enumerate(
                    (jnp.where(lane >= off, z0, zero), jnp.where(lane >= off, z1, z0), jnp.where(lane >= off, zero, z1))
                ):
                    here = (comp, c0 + b, pl.ds(r + q, H, stride=2), slice(None))
                    upd_ref[here] = upd_ref[here] + val
        return carry

    lax.fori_loop(0, total, step, 0)
    if last:
        for comp in range(2):
            for b in range(2):
                lanes = slice(b * H, (b + 1) * H)
                for q in range(2):
                    lanes_buf[comp, b, pl.ds(q, H, stride=2), :] = psum_ref[comp, q * H : (q + 1) * H, lanes]
                psum_ref[comp, :, lanes] = lanes_buf[comp, b]


def run_slots(rule, places, pieces, state, last, scalars, amplitudes, tables):
    smem = pl.BlockSpec(memory_space=pltpu.SMEM)
    vmem = pl.BlockSpec(memory_space=pltpu.VMEM)
    hbm = pl.BlockSpec(memory_space=pl.ANY)
    far = pl.BlockSpec(memory_space=pltpu.HBM)
    first = len(state) == 1
    shapes = [(2, WIDE // H, WIDE, H)] * 2 + [(2, N, N)] * 2
    at = 8 + len(pieces)
    return pl.pallas_call(
        functools.partial(slots_kernel, rule, places, first, last),
        out_shape=tuple(jax.ShapeDtypeStruct(shape, jnp.float32) for shape in shapes),
        in_specs=[smem] * 3 + [far] + [vmem] * 4 + [hbm] * len(pieces) + ([hbm] if first else [vmem] * 4),
        out_specs=(vmem,) * 4,
        input_output_aliases={} if first else {at + i: i for i in range(4)},
        scratch_shapes=[
            pltpu.VMEM((2, N, N), jnp.float32),
            pltpu.VMEM((2, N, N), jnp.bfloat16),
            pltpu.VMEM((2, N, N), jnp.float32),
            pltpu.VMEM((N, 2 * N), jnp.bfloat16),
            pltpu.VMEM((2, N, N), jnp.bfloat16),
            pltpu.VMEM((N, 2 * N), jnp.bfloat16),
            pltpu.VMEM((2, N, N), jnp.bfloat16),
            pltpu.VMEM((2, 2, N, H), jnp.float32),
            pltpu.SMEM((40,), jnp.int32),
            pltpu.SemaphoreType.DMA((2 + sum(p.shape[2] // H for p in pieces),)),
            pltpu.SemaphoreType.DMA((2,)),
        ],
        compiler_params=pltpu.CompilerParams(vmem_limit_bytes=LIMIT),
        cost_estimate=pl.CostEstimate(flops=10_000_000_000, bytes_accessed=4_000_000, transcendentals=0),
    )(*scalars, amplitudes, *tables, *pieces, *state)


def passed_along(block, axis, distance):
    devices = range(lax.axis_size(axis))
    route = [(i - distance, i) for i in devices if i - distance in devices]
    return lax.ppermute(block, axis, route)


def exchange_kernel(
    upd_ref, obj_ref, sum_ref, probe_ref, out_ref, grad_ref,
    from_left, from_above, corner, pair_in, part, x_in, piece, tile_in, gathered,
    right_send, right_recv, low_send, low_recv, pair_send, pair_recv, x_send, x_recv,
    t_send, t_recv, tg_send, tg_recv, xg_send, xg_recv, cg_send, cg_recv,
):
    p = lax.axis_index("pos")
    t = lax.axis_index("tile")
    x, z, core = p // 8, (p // 2) % 4, p % 2
    g = z * 4 + t

    def pos_of(xx, zz, cc):
        return xx * 8 + zz * 2 + cc

    right = {"pos": (p + 1) % 32, "tile": t}
    left = {"pos": (p + 31) % 32, "tile": t}
    below = {"pos": p, "tile": (t + 1) % 4}
    partner = {"pos": pos_of(x, z, 1 - core), "tile": t}
    x_peers = [{"pos": pos_of((x + d) % 4, z, core), "tile": t} for d in (1, 2, 3)]
    g_peers = [{"pos": pos_of(x, ((g + d) % 16) // 4, core), "tile": (g + d) % 4} for d in range(1, 16)]

    barrier = pltpu.get_barrier_semaphore()
    for peer in [right, left, partner] + x_peers + g_peers:
        pl.semaphore_signal(barrier, inc=1, device_id=peer, device_id_type=pl.DeviceIdType.MESH)
    pl.semaphore_wait(barrier, 21)

    started = []

    def send(source, target, send_sem, recv_sem, peer):
        copy = pltpu.make_async_remote_copy(
            src_ref=source, dst_ref=target, send_sem=send_sem, recv_sem=recv_sem,
            device_id=peer, device_id_type=pl.DeviceIdType.MESH,
        )
        copy.start()
        started.append(copy)
        return copy

    edge = send(upd_ref.at[:, 4:6, 2 * N :, :], from_left.at[:, :, 2 * N :, :], right_send.at[0], right_recv.at[0], right)
    low1 = send(upd_ref.at[:, 2:4, 2 * N :, :], from_above.at[:, 2:4], low_send.at[0], low_recv.at[0], below)
    half = send(sum_ref.at[pl.ds((1 - core) * N, N)], pair_in, pair_send.at[0], pair_recv.at[0], partner)
    mid = send(upd_ref.at[:, 4:6, N : 2 * N, :], from_left.at[:, :, N : 2 * N, :], right_send.at[1], right_recv.at[1], right)

    half.wait_recv()
    part[...] = sum_ref[pl.ds(core * N, N), :] + pair_in[...]
    x_copies = [
        send(part.at[pl.ds(((x + d) % 4) * 64, 64)], x_in.at[d - 1], x_send.at[d - 1], x_recv.at[d - 1], x_peers[d - 1])
        for d in (1, 2, 3)
    ]

    edge.wait_recv()
    has_left = (p > 0).astype(jnp.float32)
    has_above = (t > 0).astype(jnp.float32)
    corner[...] = upd_ref[:, 0:2, 2 * N :, :] + from_left[:, :, 2 * N :, :] * has_left

    for copy in x_copies:
        copy.wait_recv()
    shard = part[pl.ds(x * 64, 64), :] + x_in[0] + x_in[1] + x_in[2]
    for rg in range(8):
        for lg in range(2):
            piece[rg * 2 + lg] = shard[rg * 8 : rg * 8 + 8, lg * H : (lg + 1) * H]
    t_copies = [
        send(piece.at[(g + d) % 16], tile_in.at[d - 1], t_send.at[d - 1], t_recv.at[d - 1], g_peers[d - 1])
        for d in range(1, 16)
    ]
    low0a = send(corner.at[:, 0], from_above.at[:, 0], low_send.at[1], low_recv.at[1], below)
    power = jnp.sum(probe_ref[...] * probe_ref[...]) * (1.0 / (N * N)) + 1e-06
    scale = 1.0 / jnp.full((1, H), power, jnp.float32)

    for copy in t_copies:
        copy.wait_recv()
    own = piece[g]
    for d in range(15):
        own = own + tile_in[d]
    slots = 128 * 32
    gathered[core, x, g] = own * np.float32(1.0 / math.sqrt(slots))
    tg_copies = [
        send(gathered.at[core, x, g], gathered.at[core, x, g], tg_send.at[d - 1], tg_recv.at[d - 1], g_peers[d - 1])
        for d in range(1, 16)
    ]

    low0b = send(corner.at[:, 1], from_above.at[:, 1], low_send.at[2], low_recv.at[2], below)
    top = send(upd_ref.at[:, 4:6, :N, :], from_left.at[:, :, :N, :], right_send.at[2], right_recv.at[2], right)

    for copy in tg_copies:
        copy.wait_recv()
    xg_copies = [
        send(gathered.at[core, x], gathered.at[core, x], xg_send.at[d - 1], xg_recv.at[d - 1], x_peers[d - 1])
        for d in (1, 2, 3)
    ]
    cg_copies = [send(gathered.at[core, x], gathered.at[core, x], cg_send.at[0], cg_recv.at[0], partner)]

    def put(b, r0, value):
        for comp in range(2):
            here = (comp, slice(r0, r0 + N), slice(b * H, (b + 1) * H))
            out_ref[here] = obj_ref[here] + value[comp] * scale

    for b in (2, 3):
        put(b, N, upd_ref[:, b, N : 2 * N, :])
    for d in (1, 2, 3):
        xg_copies[d - 1].wait_recv()
        came = (x + 4 - d) % 4
        cg_copies.append(
            send(gathered.at[core, came], gathered.at[core, came], cg_send.at[d], cg_recv.at[d], partner)
        )
    mid.wait_recv()
    for b in (0, 1):
        put(b, N, upd_ref[:, b, N : 2 * N, :] + from_left[:, b, N : 2 * N, :] * has_left)
    low1.wait_recv()
    for b in (2, 3):
        put(b, 0, upd_ref[:, b, :N, :] + from_above[:, b] * has_above)
    top.wait_recv()
    for copy in cg_copies:
        copy.wait_recv()
    for h in range(2):
        for xx in range(4):
            for rg in range(8):
                for lg in range(2):
                    grad_ref[h, xx * 64 + rg * 8 : xx * 64 + rg * 8 + 8, lg * H : (lg + 1) * H] = gathered[h, xx, rg * 2 + lg]
    low0a.wait_recv()
    low0b.wait_recv()
    for b in (0, 1):
        put(b, 0, upd_ref[:, b, :N, :] + from_left[:, b, :N, :] * has_left + from_above[:, b] * has_above)
    for copy in started:
        copy.wait_send()


def exchange(update, object_field, total, probe):
    vmem = pl.BlockSpec(memory_space=pltpu.VMEM)
    f32 = jnp.float32
    dma = pltpu.SemaphoreType.DMA
    return pl.pallas_call(
        exchange_kernel,
        out_shape=(
            jax.ShapeDtypeStruct((2, BLOCK, BLOCK), f32),
            jax.ShapeDtypeStruct((2, N, N), f32),
        ),
        in_specs=[vmem] * 4,
        out_specs=(vmem, vmem),
        scratch_shapes=[
            pltpu.VMEM((2, 2, WIDE, H), f32),
            pltpu.VMEM((2, 4, N, H), f32),
            pltpu.VMEM((2, 2, N, H), f32),
            pltpu.VMEM((N, N), f32),
            pltpu.VMEM((N, N), f32),
            pltpu.VMEM((3, 64, N), f32),
            pltpu.VMEM((16, 8, H), f32),
            pltpu.VMEM((15, 8, H), f32),
            pltpu.VMEM((2, 4, 16, 8, H), f32),
            dma((3,)), dma((3,)), dma((3,)), dma((3,)), dma((1,)), dma((1,)), dma((3,)), dma((3,)),
            dma((15,)), dma((15,)), dma((15,)), dma((15,)), dma((3,)), dma((3,)), dma((4,)), dma((4,)),
        ],
        compiler_params=pltpu.CompilerParams(
            collective_id=0, has_side_effects=True, vmem_limit_bytes=32 * 1024 * 1024
        ),
    )(update, object_field, total, probe)


def shards(object_field, probe, amplitudes, corner_rows, corner_cols, counts):
    tables = [jnp.asarray(t) for t in stage_tables()]
    low_a = passed_along(object_field[:, :N, :N], "tile", -1)
    corner = passed_along(low_a, "pos", -1)
    right = passed_along(object_field[:, :, :N], "pos", -1)
    low_b = passed_along(object_field[:, :N, N:], "tile", -1)
    fixed = ((corner_rows, corner_cols, counts), amplitudes, tables)
    reach = BLOCK - N
    state = run_slots(
        lambda r, c: r <= reach, ((0, 0), (0, BLOCK), (BLOCK, 0)), (object_field, right, low_a), (probe,), False, *fixed
    )
    _, update, total, _ = run_slots(
        lambda r, c: r > reach, ((BLOCK, N), (BLOCK, BLOCK)), (low_b, corner), state, True, *fixed
    )
    return exchange(update, object_field, total.reshape(2 * N, N), probe)


def solution(mesh):
    return jax.shard_map(
        shards,
        mesh=mesh,
        in_specs=(
            P(None, "tile", "pos"),
            P(),
            P("tile", "pos", None, None, None),
            P("tile", "pos", None),
            P("tile", "pos", None),
            P("tile", "pos"),
        ),
        out_specs=(P(None, "tile", "pos"), P()),
        check_vma=False,
    )
```

profile of v0, /device:TPU:1, one launch (start us, length us, event | category | flops | bytes accessed | tf_op | source)
XLA Modules:
  0.0 127.0 jit_solution(11650585413328688366)
XLA Ops:
  0.6 0.0 copy-start.5
  0.6 0.0 copy-start.7
  0.7 0.0 copy-start.6
  0.7 0.0 copy-start.8
  0.7 0.0 copy-start
  0.7 0.0 copy-start.4
  0.7 0.0 copy-start.3
  0.7 0.0 copy-start.1
  0.7 1.4 %slice.11 = f32[2,512,256]{2,1,0:T(8,128)S(1)} slice(f32[2,512,512]{2,1,0:T(8,128)} %obj_ref.1), slice={[0:2], [0:512], [0:256]} | slice | bytes 2097152 | tf_op jit(solution)/shard_map/slice | solution.py:380
  2.2 3.4 %collective-permute-start.3 = (f32[2,512,256]{2,1,0:T(8,128)S(1)}, f32[2,512,256]{2,1,0:T(8,128)S(1)}, u32[]{:S(2)}, u32[]{:S(2)}) collective-permute-start(f32[2,512,256]{2,1,0:T(8,128)S(1)} %slice.11), channel_id=1, source_target_pairs={{4,0},{8,4},{12,8},{16,12},{20,16},{24,20},{28,24},{32,28},{36,32}... | collective-permute-start | bytes 3145736 | tf_op jit(solution)/shard_map/ppermute | solution.py:216
  5.6 1.3 %fusion = (f32[2,256,256]{2,1,0:T(8,128)S(1)}, f32[2,256,256]{2,1,0:T(8,128)S(1)}) fusion(f32[2,512,512]{2,1,0:T(8,128)} %obj_ref.1), kind=kLoop, calls=%fused_computation | loop fusion | bytes 2097152 | tf_op jit(solution)/shard_map/slice | solution.py:378
  6.9 1.3 %collective-permute-start.1 = (f32[2,256,256]{2,1,0:T(8,128)S(1)}, f32[2,256,256]{2,1,0:T(8,128)S(1)}, u32[]{:S(2)}, u32[]{:S(2)}) collective-permute-start(f32[2,256,256]{2,1,0:T(8,128)S(1)} %get-tuple-element.14), channel_id=1, source_target_pairs={{1,0},{2,1},{3,2},{5,4},{6,5},{7,6},{9,8},{10,9},{11,10},{13,12},{... | collective-permute-start | bytes 1572872 | tf_op jit(solution)/shard_map/ppermute | solution.py:216
  8.2 1.3 %collective-permute-start = (f32[2,256,256]{2,1,0:T(8,128)S(1)}, f32[2,256,256]{2,1,0:T(8,128)S(1)}, u32[]{:S(2)}, u32[]{:S(2)}) collective-permute-start(f32[2,256,256]{2,1,0:T(8,128)S(1)} %get-tuple-element.15), channel_id=1, source_target_pairs={{1,0},{2,1},{3,2},{5,4},{6,5},{7,6},{9,8},{10,9},{11,10},{13,12},{... | collective-permute-start | bytes 1572872 | tf_op jit(solution)/shard_map/ppermute | solution.py:216
  10.1 12.6 %collective-permute-done.1.refs_2_ = f32[2,256,256]{2,1,0:T(8,128)S(1)} collective-permute-done((f32[2,256,256]{2,1,0:T(8,128)S(1)}, f32[2,256,256]{2,1,0:T(8,128)S(1)}, u32[]{:S(2)}, u32[]{:S(2)}) %collective-permute-start.1) | collective-permute-done | bytes 524320 | tf_op jit(solution)/shard_map/ppermute | solution.py:216
  22.7 2.0 %collective-permute-start.2 = (f32[2,256,256]{2,1,0:T(8,128)S(1)}, f32[2,256,256]{2,1,0:T(8,128)S(1)}, u32[]{:S(2)}, u32[]{:S(2)}) collective-permute-start(f32[2,256,256]{2,1,0:T(8,128)S(1)} %collective-permute-done.1.refs_2_), channel_id=1, source_target_pairs={{4,0},{8,4},{12,8},{16,12},{20,16},{24,20},{28,24},{32,28},{36,32}... | collective-permute-start | bytes 1572872 | tf_op jit(solution)/shard_map/ppermute | solution.py:216
  24.7 0.0 collective-permute-done.3.refs_1_
  24.7 0.0 copy-done.5
  24.7 0.0 copy-done.7
  24.8 0.0 copy-done.6
  24.8 0.0 copy-done.8
  24.8 0.0 copy-done
  24.8 0.0 copy-done.4
  24.8 0.0 copy-done.3
  24.8 0.0 copy-start.2
  24.8 2.2 %copy-done.2 = bf16[1,1,32,256,256]{4,3,2,1,0:T(8,128)(2,1)S(1)} copy-done((bf16[1,1,32,256,256]{4,3,2,1,0:T(8,128)(2,1)S(1)}, bf16[1,1,32,256,256]{4,3,2,1,0:T(8,128)(2,1)}, u32[]{:S(2)}) %copy-start.2) | copy-done | bytes 4194328
  27.0 15.4 %shard_map.113 = (f32[2,6,768,128]{3,2,1,0:T(8,128)S(1)}, f32[2,6,768,128]{3,2,1,0:T(8,128)S(1)}, f32[2,256,256]{2,1,0:T(8,128)S(1)}, f32[2,256,256]{2,1,0:T(8,128)S(1)}) custom-call(s32[1,1,32]{2,1,0:T(1,128)S(1)} %copy-done.3, s32[1,1,32]{2,1,0:T(1,128)S(1)} %copy-done.4, s32[1,1]{1,0:T(1,128)S(6)} %copy.22.count_ref, ...), custom_call_target="tpu_custom_call" | custom-call | flops 10000000000 | bytes 4000000 | tf_op jit(solution)/shard_map/pallas_call | solution.py:189
  42.5 0.0 collective-permute-done.refs_0_
  42.5 0.0 collective-permute-done.2.refs_1_
  42.5 14.8 %shard_map.114 = (f32[2,6,768,128]{3,2,1,0:T(8,128)S(1)}, f32[2,6,768,128]{3,2,1,0:T(8,128)S(1)}, f32[2,256,256]{2,1,0:T(8,128)S(1)}, f32[2,256,256]{2,1,0:T(8,128)S(1)}) custom-call(s32[1,1,32]{2,1,0:T(1,128)S(1)} %copy-done.3, s32[1,1,32]{2,1,0:T(1,128)S(1)} %copy-done.4, ...), custom_call_target="tpu_custom_call", output_to_operand_aliasing={{0}: (10, {}), {1}: (11, {}), {2}: (12, {}), {3}: (13, {})} | custom-call | flops 10000000000 | bytes 4000000 | tf_op jit(solution)/shard_map/pallas_call | solution.py:189
  57.2 67.7 %shard_map.115 = (f32[2,512,512]{2,1,0:T(8,128)S(1)}, f32[2,256,256]{2,1,0:T(8,128)S(1)}) custom-call(f32[2,6,768,128]{3,2,1,0:T(8,128)S(1)} %get-tuple-element.12.upd_ref, f32[2,512,512]{2,1,0:T(8,128)S(1)} %copy-done, f32[512,256]{1,0:T(8,128)S(1)} %bitcast.1, f32[2,256,256]{2,1,0:T(8,128)S(1)} %copy-done.1), custom_call_target="tpu_custom_call" | custom-call | tf_op jit(solution)/shard_map/pallas_call | solution.py:349
  124.9 1.3 %copy.23 = f32[2,512,512]{2,1,0:T(8,128)} copy(f32[2,512,512]{2,1,0:T(8,128)S(1)} %get-tuple-element.18) | data formatting | bytes 4194304
  126.2 0.8 copy.24
  (1 shorter events, 0.0 us)
Async XLA Ops:
  0.6 24.1 %copy-start.5 = (bf16[512,512]{1,0:T(8,128)(2,1)S(1)}, bf16[512,512]{1,0:T(8,128)(2,1)}, u32[]{:S(2)}) copy-start(bf16[512,512]{1,0:T(8,128)(2,1)} %constant.11.clone.t4_ref) | copy-start | bytes 1572868
  0.6 24.1 %copy-start.7 = (bf16[2,256,256]{2,1,0:T(8,128)(2,1)S(1)}, bf16[2,256,256]{2,1,0:T(8,128)(2,1)}, u32[]{:S(2)}) copy-start(bf16[2,256,256]{2,1,0:T(8,128)(2,1)} %constant.10.clone.t3_ref) | copy-start | bytes 786436
  0.7 24.1 %copy-start.6 = (bf16[512,512]{1,0:T(8,128)(2,1)S(1)}, bf16[512,512]{1,0:T(8,128)(2,1)}, u32[]{:S(2)}) copy-start(bf16[512,512]{1,0:T(8,128)(2,1)} %constant.9.clone.t2_ref) | copy-start | bytes 1572868
  0.7 24.1 %copy-start.8 = (bf16[2,256,256]{2,1,0:T(8,128)(2,1)S(1)}, bf16[2,256,256]{2,1,0:T(8,128)(2,1)}, u32[]{:S(2)}) copy-start(bf16[2,256,256]{2,1,0:T(8,128)(2,1)} %constant.8.clone.t1_ref) | copy-start | bytes 786436
  0.7 24.1 %copy-start = (f32[2,512,512]{2,1,0:T(8,128)S(1)}, f32[2,512,512]{2,1,0:T(8,128)}, u32[]{:S(2)}) copy-start(f32[2,512,512]{2,1,0:T(8,128)} %obj_ref.1) | copy-start | bytes 6291460
  0.7 24.1 %copy-start.4 = (s32[1,1,32]{2,1,0:T(1,128)S(1)}, s32[1,1,32]{2,1,0:T(1,128)}, u32[]{:S(2)}) copy-start(s32[1,1,32]{2,1,0:T(1,128)} %cols_ref.3) | copy-start | bytes 388
  0.7 24.1 %copy-start.3 = (s32[1,1,32]{2,1,0:T(1,128)S(1)}, s32[1,1,32]{2,1,0:T(1,128)}, u32[]{:S(2)}) copy-start(s32[1,1,32]{2,1,0:T(1,128)} %rows_ref.3) | copy-start | bytes 388
  0.7 24.1 %copy-start.1 = (f32[2,256,256]{2,1,0:T(8,128)S(1)}, f32[2,256,256]{2,1,0:T(8,128)}, u32[]{:S(2)}) copy-start(f32[2,256,256]{2,1,0:T(8,128)} %probe_ref.1) | copy-start | bytes 1572868
  2.2 22.6 %collective-permute-start.3 = (f32[2,512,256]{2,1,0:T(8,128)S(1)}, f32[2,512,256]{2,1,0:T(8,128)S(1)}, u32[]{:S(2)}, u32[]{:S(2)}) collective-permute-start(f32[2,512,256]{2,1,0:T(8,128)S(1)} %slice.11), channel_id=1, source_target_pairs={{4,0},{8,4},{12,8},{16,12},{20,16},{24,20},{28,24},{32,28},{36,32}... | collective-permute-start | bytes 3145736 | tf_op jit(solution)/shard_map/ppermute | solution.py:216
  6.9 15.8 %collective-permute-start.1 = (f32[2,256,256]{2,1,0:T(8,128)S(1)}, f32[2,256,256]{2,1,0:T(8,128)S(1)}, u32[]{:S(2)}, u32[]{:S(2)}) collective-permute-start(f32[2,256,256]{2,1,0:T(8,128)S(1)} %get-tuple-element.14), channel_id=1, source_target_pairs={{1,0},{2,1},{3,2},{5,4},{6,5},{7,6},{9,8},{10,9},{11,10},{13,12},{... | collective-permute-start | bytes 1572872 | tf_op jit(solution)/shard_map/ppermute | solution.py:216
  8.2 34.3 %collective-permute-start = (f32[2,256,256]{2,1,0:T(8,128)S(1)}, f32[2,256,256]{2,1,0:T(8,128)S(1)}, u32[]{:S(2)}, u32[]{:S(2)}) collective-permute-start(f32[2,256,256]{2,1,0:T(8,128)S(1)} %get-tuple-element.15), channel_id=1, source_target_pairs={{1,0},{2,1},{3,2},{5,4},{6,5},{7,6},{9,8},{10,9},{11,10},{13,12},{... | collective-permute-start | bytes 1572872 | tf_op jit(solution)/shard_map/ppermute | solution.py:216
  22.7 19.7 %collective-permute-start.2 = (f32[2,256,256]{2,1,0:T(8,128)S(1)}, f32[2,256,256]{2,1,0:T(8,128)S(1)}, u32[]{:S(2)}, u32[]{:S(2)}) collective-permute-start(f32[2,256,256]{2,1,0:T(8,128)S(1)} %collective-permute-done.1.refs_2_), channel_id=1, source_target_pairs={{4,0},{8,4},{12,8},{16,12},{20,16},{24,20},{28,24},{32,28},{36,32}... | collective-permute-start | bytes 1572872 | tf_op jit(solution)/shard_map/ppermute | solution.py:216
  24.8 2.2 %copy-start.2 = (bf16[1,1,32,256,256]{4,3,2,1,0:T(8,128)(2,1)S(1)}, bf16[1,1,32,256,256]{4,3,2,1,0:T(8,128)(2,1)}, u32[]{:S(2)}) copy-start(bf16[1,1,32,256,256]{4,3,2,1,0:T(8,128)(2,1)} %amp_ref.3) | copy-start | bytes 12582916
where the time goes:
time: 127 us
  Pallas kernels  97.9 us (77%)
  waiting for transfers between devices  12.6 us (10%)
  starting transfers between devices  7.98 us (6%)
  local copies, waits for them, and re-layouts  7.08 us (6%)
  between operations  1.5 us (1%)
    pallas_call x1, Pallas kernels, exchange(): pl.pallas_call(exchange_kernel, out_shape=(jax.ShapeDtypeStruct((2, BLOCK...  67.7 us
    pallas_call x2, Pallas kernels, run_slots(): pl.pallas_call(functools.partial(slots_kernel, rule, places, first, last)...  30.2 us
    ppermute x4, waiting for transfers between devices, passed_along(): return lax.ppermute(block, axis, route)  12.6 us
    ppermute x4, starting transfers between devices, passed_along(): return lax.ppermute(block, axis, route)  7.98 us
    unnamed x20, local copies, waits for them, and re-layouts  4.34 us
  transfers between devices with their start and end apart: 4, of which 1 were waited for; matrix products, arithmetic and copies ran while one was open for 1% of the time, Pallas kernels for 12%

commit v1 on v0

--- a/solution.py
+++ b/solution.py
@@ -49,7 +49,8 @@
         probe_ref = refs[0]
     refs = refs[1 if first else 4 :]
     ext, upd_ref, psum_ref, prb = refs[:4]
-    (pat, ext_b, exit_s, near_b, fold_b, back_b, amp_buf, lanes_buf, order, piece_sem, amp_sem) = refs[4:]
+    pat, ext_b, exit_s, amp_buf = (refs[4 + 4 * i : 8 + 4 * i] for i in range(4))
+    near_b, fold_b, back_b, lanes_buf, order, piece_sem, amp_sem = refs[20:]
     copies = []
 
     def bring(source, target):
@@ -68,13 +69,8 @@
 
     total = lax.fori_loop(0, rows_ref.shape[2], collect, jnp.int32(0))
 
-    def amp_copy(i):
-        slot = lax.rem(i, 2)
-        return pltpu.make_async_copy(amp_ref.at[0, 0, order[i]], amp_buf.at[slot], amp_sem.at[slot])
-
-    @pl.when(total > 0)
-    def _():
-        amp_copy(0).start()
+    def amp_copy(i, k=0):
+        return pltpu.make_async_copy(amp_ref.at[0, 0, order[i]], amp_buf[k], amp_sem.at[k])
 
     if first:
         for b in range(2):
@@ -91,84 +87,133 @@
 
     lane = lax.broadcasted_iota(jnp.int32, (H, H), 1)
 
-    def step(i, carry):
+    dot = functools.partial(jnp.dot, preferred_element_type=jnp.float32)
+
+    def place(i):
         s = order[i]
-        r = rows_ref[0, 0, s]
         c = cols_ref[0, 0, s]
-        off = lax.rem(c, H)
-        c0 = c // H
+        return rows_ref[0, 0, s], c // H, lax.rem(c, H)
+
+    def enter(i, k, q):
+        r, c0, off = place(i)
         back_shift = lax.rem(H - off, H)
-
-        @pl.when(i + 1 < total)
-        def _():
-            amp_copy(i + 1).start()
-
-        for q in range(2):
-            part = []
-            for comp in range(2):
-                blocks = [
-                    pltpu.roll(ext[comp, c0 + b, pl.ds(r + q, H, stride=2), :], back_shift, 1)
-                    for b in range(3)
-                ]
-                part.append(
-                    [jnp.where(lane < H - off, blocks[b], blocks[b + 1]) for b in range(2)]
-                )
-            for b in range(2):
-                here = (slice(q * H, (q + 1) * H), slice(b * H, (b + 1) * H))
-                pre, pim = prb[0][here], prb[1][here]
-                are, aim = part[0][b], part[1][b]
-                ere = pre * are - pim * aim
-                eim = pre * aim + pim * are
-                pat[(0,) + here] = are
-                pat[(1,) + here] = aim
-                exit_s[(0,) + here] = ere
-                exit_s[(1,) + here] = eim
-                ext_b[q, 0:H, b * H : (b + 1) * H] = ere.astype(jnp.bfloat16)
-                ext_b[q, H:N, b * H : (b + 1) * H] = eim.astype(jnp.bfloat16)
-
-        dot = functools.partial(jnp.dot, preferred_element_type=jnp.float32)
-        even = dot(t1_ref[0], ext_b[0])
-        odd = dot(t1_ref[1], ext_b[1])
+        keep = lane < H - off
+        part = []
+        for comp in range(2):
+            blocks = [pltpu.roll(ext[comp, c0 + b, pl.ds(r + q, H, stride=2), :], back_shift, 1) for b in range(3)]
+            part.append([jnp.where(keep, blocks[b], blocks[b + 1]) for b in range(2)])
+        for b in range(2):
+            here = (slice(q * H, (q + 1) * H), slice(b * H, (b + 1) * H))
+            pre, pim = prb[(0,) + here], prb[(1,) + here]
+            are, aim = part[0][b], part[1][b]
+            ere = pre * are - pim * aim
+            eim = pre * aim + pim * are
+            pat[k][(0,) + here] = are
+            pat[k][(1,) + here] = aim
+            exit_s[k][(0,) + here] = ere
+            exit_s[k][(1,) + here] = eim
+            ext_b[k][q, 0:H, b * H : (b + 1) * H] = ere.astype(jnp.bfloat16)
+            ext_b[k][q, H:N, b * H : (b + 1) * H] = eim.astype(jnp.bfloat16)
+
+    def near(k, m):
+        even = dot(t1_ref[0], ext_b[k][0])
+        odd = dot(t1_ref[1], ext_b[k][1])
         for comp in range(2):
             e, o = even[comp * H : (comp + 1) * H], odd[comp * H : (comp + 1) * H]
-            near_b[0:H, comp * N : (comp + 1) * N] = (e + o).astype(jnp.bfloat16)
-            near_b[H:N, comp * N : (comp + 1) * N] = (e - o).astype(jnp.bfloat16)
-
-        amp_copy(i).wait()
-        amp = amp_buf.at[lax.rem(i, 2)]
-        far = dot(near_b[...], t2_ref[...])
+            near_b[m, 0:H, comp * N : (comp + 1) * N] = (e + o).astype(jnp.bfloat16)
+            near_b[m, H:N, comp * N : (comp + 1) * N] = (e - o).astype(jnp.bfloat16)
+
+    def project(k, m):
+        far = dot(near_b[m], t2_ref[...])
         fre, fim = far[:, :N], far[:, N:]
-        ratio = amp[...].astype(jnp.float32) * lax.rsqrt(fre * fre + fim * fim + 0.25)
+        ratio = amp_buf[k][...].astype(jnp.float32) * lax.rsqrt(fre * fre + fim * fim + 0.25)
         for comp, part in enumerate((fre * ratio, fim * ratio)):
             top, low = part[:H], part[H:]
-            fold_b[0, comp * H : (comp + 1) * H, :] = (top + low).astype(jnp.bfloat16)
-            fold_b[1, comp * H : (comp + 1) * H, :] = (top - low).astype(jnp.bfloat16)
-
-        for q in range(2):
-            back = dot(t3_ref[q], fold_b[q])
-            for comp in range(2):
-                back_b[q * H : (q + 1) * H, comp * N : (comp + 1) * N] = back[comp * H : (comp + 1) * H].astype(
-                    jnp.bfloat16
-                )
-        new = dot(back_b[...], t4_ref[...])
-        dre = new[:, :N] - exit_s[0]
-        dim = new[:, N:] - exit_s[1]
-        psum_ref[0] += pat[0] * dre + pat[1] * dim
-        psum_ref[1] += pat[0] * dim - pat[1] * dre
-        terms = (prb[0] * dre + prb[1] * dim, prb[0] * dim - prb[1] * dre)
-        for comp in range(2):
+            fold_b[m, 0, comp * H : (comp + 1) * H, :] = (top + low).astype(jnp.bfloat16)
+            fold_b[m, 1, comp * H : (comp + 1) * H, :] = (top - low).astype(jnp.bfloat16)
+
+    def back(k, m, q):
+        part = dot(t3_ref[q], fold_b[m, q])
+        for comp in range(2):
+            back_b[m, q * H : (q + 1) * H, comp * N : (comp + 1) * N] = part[comp * H : (comp + 1) * H].astype(
+                jnp.bfloat16
+            )
+
+    def finish(i, k, m, q, live):
+        r, c0, off = place(i)
+        here = slice(q * H, (q + 1) * H)
+        new = dot(back_b[m, here], t4_ref[...])
+        dre = new[:, :N] - exit_s[k][0, here]
+        dim = new[:, N:] - exit_s[k][1, here]
+        if live is not None:
+            dre, dim = dre * live, dim * live
+        psum_ref[0, here] += pat[k][0, here] * dre + pat[k][1, here] * dim
+        psum_ref[1, here] += pat[k][0, here] * dim - pat[k][1, here] * dre
+        pre, pim = prb[0, here], prb[1, here]
+        terms = (pre * dre + pim * dim, pre * dim - pim * dre)
+        for comp in range(2):
+            z0 = pltpu.roll(terms[comp][:, :H], off, 1)
+            z1 = pltpu.roll(terms[comp][:, H:], off, 1)
+            zero = jnp.zeros_like(z0)
+            keep = lane >= off
+            for b, val in enumerate((jnp.where(keep, z0, zero), jnp.where(keep, z1, z0), jnp.where(keep, zero, z1))):
+                spot = (comp, c0 + b, pl.ds(r + q, H, stride=2), slice(None))
+                upd_ref[spot] = upd_ref[spot] + val
+
+    final = jnp.maximum(total - 1, 0)
+    pairs = (total + 1) // 2
+
+    def fetch(pair, half):
+        for m in range(2):
+            amp_copy(jnp.minimum(2 * pair + m, final), 2 * half + m).start()
+
+    def work(pair, half):
+        follow = jnp.minimum(pair + 1, pairs - 1)
+        ids = [jnp.minimum(2 * pair + m, final) for m in range(2)]
+        nxt = [jnp.minimum(2 * follow + m, final) for m in range(2)]
+        live = (2 * pair + 1 < total).astype(jnp.float32)
+        for m in range(2):
+            amp_copy(ids[m], 2 * half + m).wait()
+        for m in range(2):
+            near(2 * half + m, m)
+        enter(nxt[0], 2 * (1 - half), 0)
+        for m in range(2):
+            project(2 * half + m, m)
+        enter(nxt[0], 2 * (1 - half), 1)
+        for m in range(2):
             for q in range(2):
-                z0 = pltpu.roll(terms[comp][q * H : (q + 1) * H, :H], off, 1)
-                z1 = pltpu.roll(terms[comp][q * H : (q + 1) * H, H:], off, 1)
-                zero = jnp.zeros_like(z0)
-                for b, val in enumerate(
-                    (jnp.where(lane >= off, z0, zero), jnp.where(lane >= off, z1, z0), jnp.where(lane >= off, zero, z1))
-                ):
-                    here = (comp, c0 + b, pl.ds(r + q, H, stride=2), slice(None))
-                    upd_ref[here] = upd_ref[here] + val
+                back(2 * half + m, m, q)
+        enter(nxt[1], 2 * (1 - half) + 1, 0)
+        for m in range(2):
+            for q in range(2):
+                finish(ids[m], 2 * half + m, m, q, live if m else None)
+        enter(nxt[1], 2 * (1 - half) + 1, 1)
+
+    @pl.when(total > 0)
+    def _():
+        fetch(0, 0)
+        for m in range(2):
+            for q in range(2):
+                enter(jnp.minimum(m, final), m, q)
+
+    def step(j, carry):
+        for half in range(2):
+            pair = 2 * j + half
+
+            def run(pair=pair, half=half):
+                @pl.when(pair + 1 < pairs)
+                def _():
+                    fetch(pair + 1, 1 - half)
+
+                work(pair, half)
+
+            if half == 0:
+                run()
+            else:
+                pl.when(pair < pairs)(run)
         return carry
 
-    lax.fori_loop(0, total, step, 0)
+    lax.fori_loop(0, (pairs + 1) // 2, step, 0)
     if last:
         for comp in range(2):
             for b in range(2):
@@ -193,17 +238,17 @@
         out_specs=(vmem,) * 4,
         input_output_aliases={} if first else {at + i: i for i in range(4)},
         scratch_shapes=[
-            pltpu.VMEM((2, N, N), jnp.float32),
-            pltpu.VMEM((2, N, N), jnp.bfloat16),
-            pltpu.VMEM((2, N, N), jnp.float32),
-            pltpu.VMEM((N, 2 * N), jnp.bfloat16),
-            pltpu.VMEM((2, N, N), jnp.bfloat16),
-            pltpu.VMEM((N, 2 * N), jnp.bfloat16),
-            pltpu.VMEM((2, N, N), jnp.bfloat16),
+            *[pltpu.VMEM((2, N, N), jnp.float32)] * 4,
+            *[pltpu.VMEM((2, N, N), jnp.bfloat16)] * 4,
+            *[pltpu.VMEM((2, N, N), jnp.float32)] * 4,
+            *[pltpu.VMEM((N, N), jnp.bfloat16)] * 4,
+            pltpu.VMEM((2, N, 2 * N), jnp.bfloat16),
+            pltpu.VMEM((2, 2, N, N), jnp.bfloat16),
+            pltpu.VMEM((2, N, 2 * N), jnp.bfloat16),
             pltpu.VMEM((2, 2, N, H), jnp.float32),
             pltpu.SMEM((40,), jnp.int32),
             pltpu.SemaphoreType.DMA((2 + sum(p.shape[2] // H for p in pieces),)),
-            pltpu.SemaphoreType.DMA((2,)),
+            pltpu.SemaphoreType.DMA((4,)),
         ],
         compiler_params=pltpu.CompilerParams(vmem_limit_bytes=LIMIT),
         cost_estimate=pl.CostEstimate(flops=10_000_000_000, bytes_accessed=4_000_000, transcendentals=0),

time: 127 us -> 111 us (0.87)
  Pallas kernels: 97.9 us -> 79.1 us
  waiting for transfers between devices: 12.6 us -> 15 us
    pallas_call x2, Pallas kernels: 30.2 us -> 8.49 us  [run_slots(): pl.pallas_call(functools.partial(slots_kernel, rule, places, first, last)...]
    pallas_call x1, Pallas kernels: 67.7 us -> 70.6 us  [exchange(): pl.pallas_call(exchange_kernel, out_shape=(jax.ShapeDtypeStruct((2, BLOCK...]
    ppermute x4, waiting for transfers between devices: 12.6 us -> 15 us  [passed_along(): return lax.ppermute(block, axis, route)]
  transfers between devices with their start and end apart: 4 -> 4, of which waited for: 1 -> 3; matrix products, arithmetic and copies ran while one was open for 1% -> 1% of each run, Pallas kernels for 12% -> 4%
where the time goes in v1:
time: 111 us
  Pallas kernels  79.1 us (71%)
  waiting for transfers between devices  15 us (14%)
  starting transfers between devices  7.98 us (7%)
  local copies, waits for them, and re-layouts  7.08 us (6%)
  between operations  1.49 us (1%)
    pallas_call x1, Pallas kernels, exchange(): pl.pallas_call(exchange_kernel, out_shape=(jax.ShapeDtypeStruct((2, BLOCK...  70.6 us
    ppermute x4, waiting for transfers between devices, passed_along(): return lax.ppermute(block, axis, route)  15 us
    pallas_call x2, Pallas kernels, run_slots(): pl.pallas_call(functools.partial(slots_kernel, rule, places, first, last)...  8.49 us
    ppermute x4, starting transfers between devices, passed_along(): return lax.ppermute(block, axis, route)  7.98 us
    unnamed x20, local copies, waits for them, and re-layouts  4.34 us
  transfers between devices with their start and end apart: 4, of which 3 were waited for; matrix products, arithmetic and copies ran while one was open for 1% of the time, Pallas kernels for 4%

profile of v1, /device:TPU:1, one launch (start us, length us, event | category | flops | bytes accessed | tf_op | source)
XLA Modules:
  0.0 110.6 jit_solution(11181441184967385429)
XLA Ops:
  0.6 0.0 copy-start.5
  0.6 0.0 copy-start.7
  0.7 0.0 copy-start.6
  0.7 0.0 copy-start.8
  0.7 0.0 copy-start
  0.7 0.0 copy-start.4
  0.7 0.0 copy-start.3
  0.7 0.0 copy-start.1
  0.7 1.4 %slice.11 = f32[2,512,256]{2,1,0:T(8,128)S(1)} slice(f32[2,512,512]{2,1,0:T(8,128)} %obj_ref.1), slice={[0:2], [0:512], [0:256]} | slice | bytes 2097152 | tf_op jit(solution)/shard_map/slice | solution.py:425
  2.2 3.4 %collective-permute-start.3 = (f32[2,512,256]{2,1,0:T(8,128)S(1)}, f32[2,512,256]{2,1,0:T(8,128)S(1)}, u32[]{:S(2)}, u32[]{:S(2)}) collective-permute-start(f32[2,512,256]{2,1,0:T(8,128)S(1)} %slice.11), channel_id=1, source_target_pairs={{4,0},{8,4},{12,8},{16,12},{20,16},{24,20},{28,24},{32,28},{36,32}... | collective-permute-start | bytes 3145736 | tf_op jit(solution)/shard_map/ppermute | solution.py:261
  5.6 1.3 %fusion = (f32[2,256,256]{2,1,0:T(8,128)S(1)}, f32[2,256,256]{2,1,0:T(8,128)S(1)}) fusion(f32[2,512,512]{2,1,0:T(8,128)} %obj_ref.1), kind=kLoop, calls=%fused_computation | loop fusion | bytes 2097152 | tf_op jit(solution)/shard_map/slice | solution.py:423
  6.9 1.3 %collective-permute-start.1 = (f32[2,256,256]{2,1,0:T(8,128)S(1)}, f32[2,256,256]{2,1,0:T(8,128)S(1)}, u32[]{:S(2)}, u32[]{:S(2)}) collective-permute-start(f32[2,256,256]{2,1,0:T(8,128)S(1)} %get-tuple-element.14), channel_id=1, source_target_pairs={{1,0},{2,1},{3,2},{5,4},{6,5},{7,6},{9,8},{10,9},{11,10},{13,12},{... | collective-permute-start | bytes 1572872 | tf_op jit(solution)/shard_map/ppermute | solution.py:261
  8.2 1.3 %collective-permute-start = (f32[2,256,256]{2,1,0:T(8,128)S(1)}, f32[2,256,256]{2,1,0:T(8,128)S(1)}, u32[]{:S(2)}, u32[]{:S(2)}) collective-permute-start(f32[2,256,256]{2,1,0:T(8,128)S(1)} %get-tuple-element.15), channel_id=1, source_target_pairs={{1,0},{2,1},{3,2},{5,4},{6,5},{7,6},{9,8},{10,9},{11,10},{13,12},{... | collective-permute-start | bytes 1572872 | tf_op jit(solution)/shard_map/ppermute | solution.py:261
  10.1 12.6 %collective-permute-done.1.refs_2_ = f32[2,256,256]{2,1,0:T(8,128)S(1)} collective-permute-done((f32[2,256,256]{2,1,0:T(8,128)S(1)}, f32[2,256,256]{2,1,0:T(8,128)S(1)}, u32[]{:S(2)}, u32[]{:S(2)}) %collective-permute-start.1) | collective-permute-done | bytes 524320 | tf_op jit(solution)/shard_map/ppermute | solution.py:261
  22.7 2.0 %collective-permute-start.2 = (f32[2,256,256]{2,1,0:T(8,128)S(1)}, f32[2,256,256]{2,1,0:T(8,128)S(1)}, u32[]{:S(2)}, u32[]{:S(2)}) collective-permute-start(f32[2,256,256]{2,1,0:T(8,128)S(1)} %collective-permute-done.1.refs_2_), channel_id=1, source_target_pairs={{4,0},{8,4},{12,8},{16,12},{20,16},{24,20},{28,24},{32,28},{36,32}... | collective-permute-start | bytes 1572872 | tf_op jit(solution)/shard_map/ppermute | solution.py:261
  24.7 0.0 collective-permute-done.3.refs_1_
  24.7 0.0 copy-done.5
  24.7 0.0 copy-done.7
  24.8 0.0 copy-done.6
  24.8 0.0 copy-done.8
  24.8 0.0 copy-done
  24.8 0.0 copy-done.4
  24.8 0.0 copy-done.3
  24.8 0.0 copy-start.2
  24.8 2.2 %copy-done.2 = bf16[1,1,32,256,256]{4,3,2,1,0:T(8,128)(2,1)S(1)} copy-done((bf16[1,1,32,256,256]{4,3,2,1,0:T(8,128)(2,1)S(1)}, bf16[1,1,32,256,256]{4,3,2,1,0:T(8,128)(2,1)}, u32[]{:S(2)}) %copy-start.2) | copy-done | bytes 4194328
  27.0 4.6 %shard_map.113 = (f32[2,6,768,128]{3,2,1,0:T(8,128)S(1)}, f32[2,6,768,128]{3,2,1,0:T(8,128)S(1)}, f32[2,256,256]{2,1,0:T(8,128)S(1)}, f32[2,256,256]{2,1,0:T(8,128)S(1)}) custom-call(s32[1,1,32]{2,1,0:T(1,128)S(1)} %copy-done.3, s32[1,1,32]{2,1,0:T(1,128)S(1)} %copy-done.4, s32[1,1]{1,0:T(1,128)S(6)} %copy.22.count_ref, ...), custom_call_target="tpu_custom_call" | custom-call | flops 10000000000 | bytes 4000000 | tf_op jit(solution)/shard_map/pallas_call | solution.py:234
  31.6 2.0 %collective-permute-done.refs_0_ = f32[2,256,256]{2,1,0:T(8,128)S(1)} collective-permute-done((f32[2,256,256]{2,1,0:T(8,128)S(1)}, f32[2,256,256]{2,1,0:T(8,128)S(1)}, u32[]{:S(2)}, u32[]{:S(2)}) %collective-permute-start) | collective-permute-done | bytes 524320 | tf_op jit(solution)/shard_map/ppermute | solution.py:261
  33.7 0.3 collective-permute-done.2.refs_1_
  34.0 3.9 %shard_map.114 = (f32[2,6,768,128]{3,2,1,0:T(8,128)S(1)}, f32[2,6,768,128]{3,2,1,0:T(8,128)S(1)}, f32[2,256,256]{2,1,0:T(8,128)S(1)}, f32[2,256,256]{2,1,0:T(8,128)S(1)}) custom-call(s32[1,1,32]{2,1,0:T(1,128)S(1)} %copy-done.3, s32[1,1,32]{2,1,0:T(1,128)S(1)} %copy-done.4, ...), custom_call_target="tpu_custom_call", output_to_operand_aliasing={{0}: (10, {}), {1}: (11, {}), {2}: (12, {}), {3}: (13, {})} | custom-call | flops 10000000000 | bytes 4000000 | tf_op jit(solution)/shard_map/pallas_call | solution.py:234
  37.9 70.6 %shard_map.115 = (f32[2,512,512]{2,1,0:T(8,128)S(1)}, f32[2,256,256]{2,1,0:T(8,128)S(1)}) custom-call(f32[2,6,768,128]{3,2,1,0:T(8,128)S(1)} %get-tuple-element.12.upd_ref, f32[2,512,512]{2,1,0:T(8,128)S(1)} %copy-done, f32[512,256]{1,0:T(8,128)S(1)} %bitcast.1, f32[2,256,256]{2,1,0:T(8,128)S(1)} %copy-done.1), custom_call_target="tpu_custom_call" | custom-call | tf_op jit(solution)/shard_map/pallas_call | solution.py:394
  108.5 1.3 %copy.23 = f32[2,512,512]{2,1,0:T(8,128)} copy(f32[2,512,512]{2,1,0:T(8,128)S(1)} %get-tuple-element.18) | data formatting | bytes 4194304
  109.8 0.8 copy.24
  (1 shorter events, 0.0 us)
Async XLA Ops:
  0.6 24.1 %copy-start.5 = (bf16[512,512]{1,0:T(8,128)(2,1)S(1)}, bf16[512,512]{1,0:T(8,128)(2,1)}, u32[]{:S(2)}) copy-start(bf16[512,512]{1,0:T(8,128)(2,1)} %constant.11.clone.t4_ref) | copy-start | bytes 1572868
  0.6 24.1 %copy-start.7 = (bf16[2,256,256]{2,1,0:T(8,128)(2,1)S(1)}, bf16[2,256,256]{2,1,0:T(8,128)(2,1)}, u32[]{:S(2)}) copy-start(bf16[2,256,256]{2,1,0:T(8,128)(2,1)} %constant.10.clone.t3_ref) | copy-start | bytes 786436
  0.7 24.1 %copy-start.6 = (bf16[512,512]{1,0:T(8,128)(2,1)S(1)}, bf16[512,512]{1,0:T(8,128)(2,1)}, u32[]{:S(2)}) copy-start(bf16[512,512]{1,0:T(8,128)(2,1)} %constant.9.clone.t2_ref) | copy-start | bytes 1572868
  0.7 24.1 %copy-start.8 = (bf16[2,256,256]{2,1,0:T(8,128)(2,1)S(1)}, bf16[2,256,256]{2,1,0:T(8,128)(2,1)}, u32[]{:S(2)}) copy-start(bf16[2,256,256]{2,1,0:T(8,128)(2,1)} %constant.8.clone.t1_ref) | copy-start | bytes 786436
  0.7 24.1 %copy-start = (f32[2,512,512]{2,1,0:T(8,128)S(1)}, f32[2,512,512]{2,1,0:T(8,128)}, u32[]{:S(2)}) copy-start(f32[2,512,512]{2,1,0:T(8,128)} %obj_ref.1) | copy-start | bytes 6291460
  0.7 24.1 %copy-start.4 = (s32[1,1,32]{2,1,0:T(1,128)S(1)}, s32[1,1,32]{2,1,0:T(1,128)}, u32[]{:S(2)}) copy-start(s32[1,1,32]{2,1,0:T(1,128)} %cols_ref.3) | copy-start | bytes 388
  0.7 24.1 %copy-start.3 = (s32[1,1,32]{2,1,0:T(1,128)S(1)}, s32[1,1,32]{2,1,0:T(1,128)}, u32[]{:S(2)}) copy-start(s32[1,1,32]{2,1,0:T(1,128)} %rows_ref.3) | copy-start | bytes 388
  0.7 24.1 %copy-start.1 = (f32[2,256,256]{2,1,0:T(8,128)S(1)}, f32[2,256,256]{2,1,0:T(8,128)}, u32[]{:S(2)}) copy-start(f32[2,256,256]{2,1,0:T(8,128)} %probe_ref.1) | copy-start | bytes 1572868
  2.2 22.6 %collective-permute-start.3 = (f32[2,512,256]{2,1,0:T(8,128)S(1)}, f32[2,512,256]{2,1,0:T(8,128)S(1)}, u32[]{:S(2)}, u32[]{:S(2)}) collective-permute-start(f32[2,512,256]{2,1,0:T(8,128)S(1)} %slice.11), channel_id=1, source_target_pairs={{4,0},{8,4},{12,8},{16,12},{20,16},{24,20},{28,24},{32,28},{36,32}... | collective-permute-start | bytes 3145736 | tf_op jit(solution)/shard_map/ppermute | solution.py:261
  6.9 15.8 %collective-permute-start.1 = (f32[2,256,256]{2,1,0:T(8,128)S(1)}, f32[2,256,256]{2,1,0:T(8,128)S(1)}, u32[]{:S(2)}, u32[]{:S(2)}) collective-permute-start(f32[2,256,256]{2,1,0:T(8,128)S(1)} %get-tuple-element.14), channel_id=1, source_target_pairs={{1,0},{2,1},{3,2},{5,4},{6,5},{7,6},{9,8},{10,9},{11,10},{13,12},{... | collective-permute-start | bytes 1572872 | tf_op jit(solution)/shard_map/ppermute | solution.py:261
  8.2 25.5 %collective-permute-start = (f32[2,256,256]{2,1,0:T(8,128)S(1)}, f32[2,256,256]{2,1,0:T(8,128)S(1)}, u32[]{:S(2)}, u32[]{:S(2)}) collective-permute-start(f32[2,256,256]{2,1,0:T(8,128)S(1)} %get-tuple-element.15), channel_id=1, source_target_pairs={{1,0},{2,1},{3,2},{5,4},{6,5},{7,6},{9,8},{10,9},{11,10},{13,12},{... | collective-permute-start | bytes 1572872 | tf_op jit(solution)/shard_map/ppermute | solution.py:261
  22.7 11.3 %collective-permute-start.2 = (f32[2,256,256]{2,1,0:T(8,128)S(1)}, f32[2,256,256]{2,1,0:T(8,128)S(1)}, u32[]{:S(2)}, u32[]{:S(2)}) collective-permute-start(f32[2,256,256]{2,1,0:T(8,128)S(1)} %collective-permute-done.1.refs_2_), channel_id=1, source_target_pairs={{4,0},{8,4},{12,8},{16,12},{20,16},{24,20},{28,24},{32,28},{36,32}... | collective-permute-start | bytes 1572872 | tf_op jit(solution)/shard_map/ppermute | solution.py:261
  24.8 2.2 %copy-start.2 = (bf16[1,1,32,256,256]{4,3,2,1,0:T(8,128)(2,1)S(1)}, bf16[1,1,32,256,256]{4,3,2,1,0:T(8,128)(2,1)}, u32[]{:S(2)}) copy-start(bf16[1,1,32,256,256]{4,3,2,1,0:T(8,128)(2,1)} %amp_ref.3) | copy-start | bytes 12582916

commit v2 on v1

--- a/solution.py
+++ b/solution.py
@@ -261,6 +261,12 @@
     return lax.ppermute(block, axis, route)
 
 
+def from_diagonal(block):
+    wide, tall = lax.axis_size("pos"), lax.axis_size("tile")
+    route = [((p + 1) * tall + t + 1, p * tall + t) for p in range(wide - 1) for t in range(tall - 1)]
+    return lax.ppermute(block, ("pos", "tile"), route)
+
+
 def exchange_kernel(
     upd_ref, obj_ref, sum_ref, probe_ref, out_ref, grad_ref,
     from_left, from_above, corner, pair_in, part, x_in, piece, tile_in, gathered,
@@ -298,22 +304,19 @@
         started.append(copy)
         return copy
 
-    edge = send(upd_ref.at[:, 4:6, 2 * N :, :], from_left.at[:, :, 2 * N :, :], right_send.at[0], right_recv.at[0], right)
     low1 = send(upd_ref.at[:, 2:4, 2 * N :, :], from_above.at[:, 2:4], low_send.at[0], low_recv.at[0], below)
     half = send(sum_ref.at[pl.ds((1 - core) * N, N)], pair_in, pair_send.at[0], pair_recv.at[0], partner)
-    mid = send(upd_ref.at[:, 4:6, N : 2 * N, :], from_left.at[:, :, N : 2 * N, :], right_send.at[1], right_recv.at[1], right)
-
     half.wait_recv()
     part[...] = sum_ref[pl.ds(core * N, N), :] + pair_in[...]
     x_copies = [
         send(part.at[pl.ds(((x + d) % 4) * 64, 64)], x_in.at[d - 1], x_send.at[d - 1], x_recv.at[d - 1], x_peers[d - 1])
         for d in (1, 2, 3)
     ]
-
-    edge.wait_recv()
+    edge = send(upd_ref.at[:, 4:6, 2 * N :, :], from_left.at[:, :, 2 * N :, :], right_send.at[0], right_recv.at[0], right)
     has_left = (p > 0).astype(jnp.float32)
     has_above = (t > 0).astype(jnp.float32)
-    corner[...] = upd_ref[:, 0:2, 2 * N :, :] + from_left[:, :, 2 * N :, :] * has_left
+    power = jnp.sum(probe_ref[...] * probe_ref[...]) * (1.0 / (N * N)) + 1e-06
+    scale = 1.0 / jnp.full((1, H), power, jnp.float32)
 
     for copy in x_copies:
         copy.wait_recv()
@@ -325,9 +328,9 @@
         send(piece.at[(g + d) % 16], tile_in.at[d - 1], t_send.at[d - 1], t_recv.at[d - 1], g_peers[d - 1])
         for d in range(1, 16)
     ]
-    low0a = send(corner.at[:, 0], from_above.at[:, 0], low_send.at[1], low_recv.at[1], below)
-    power = jnp.sum(probe_ref[...] * probe_ref[...]) * (1.0 / (N * N)) + 1e-06
-    scale = 1.0 / jnp.full((1, H), power, jnp.float32)
+    mid = send(upd_ref.at[:, 4:6, N : 2 * N, :], from_left.at[:, :, N : 2 * N, :], right_send.at[1], right_recv.at[1], right)
+    edge.wait_recv()
+    corner[...] = upd_ref[:, 0:2, 2 * N :, :] + from_left[:, :, 2 * N :, :] * has_left
 
     for copy in t_copies:
         copy.wait_recv()
@@ -340,7 +343,7 @@
         send(gathered.at[core, x, g], gathered.at[core, x, g], tg_send.at[d - 1], tg_recv.at[d - 1], g_peers[d - 1])
         for d in range(1, 16)
     ]
-
+    low0a = send(corner.at[:, 0], from_above.at[:, 0], low_send.at[1], low_recv.at[1], below)
     low0b = send(corner.at[:, 1], from_above.at[:, 1], low_send.at[2], low_recv.at[2], below)
     top = send(upd_ref.at[:, 4:6, :N, :], from_left.at[:, :, :N, :], right_send.at[2], right_recv.at[2], right)
 
@@ -420,18 +423,22 @@
 
 def shards(object_field, probe, amplitudes, corner_rows, corner_cols, counts):
     tables = [jnp.asarray(t) for t in stage_tables()]
-    low_a = passed_along(object_field[:, :N, :N], "tile", -1)
-    corner = passed_along(low_a, "pos", -1)
+    lows, corners = [], []
+    for q in range(2):
+        rows = slice(q * H, (q + 1) * H)
+        lows.append(passed_along(object_field[:, rows, :], "tile", -1))
+        corners.append(from_diagonal(object_field[:, rows, :N]))
     right = passed_along(object_field[:, :, :N], "pos", -1)
-    low_b = passed_along(object_field[:, :N, N:], "tile", -1)
     fixed = ((corner_rows, corner_cols, counts), amplitudes, tables)
     reach = BLOCK - N
     state = run_slots(
-        lambda r, c: r <= reach, ((0, 0), (0, BLOCK), (BLOCK, 0)), (object_field, right, low_a), (probe,), False, *fixed
+        lambda r, c: (r <= reach) & (c <= reach), ((0, 0),), (object_field,), (probe,), False, *fixed
     )
-    _, update, total, _ = run_slots(
-        lambda r, c: r > reach, ((BLOCK, N), (BLOCK, BLOCK)), (low_b, corner), state, True, *fixed
-    )
+    state = run_slots(lambda r, c: (r <= reach) & (c > reach), ((0, BLOCK),), (right,), state, False, *fixed)
+    for q, rule in enumerate((lambda r, c: (r > reach) & (r <= reach + H), lambda r, c: r > reach + H)):
+        row = BLOCK + q * H
+        state = run_slots(rule, ((row, 0), (row, BLOCK)), (lows[q], corners[q]), state, q == 1, *fixed)
+    _, update, total, _ = state
     return exchange(update, object_field, total.reshape(2 * N, N), probe)
 
 

time: 111 us -> 106 us (0.955)
  waiting for transfers between devices: 15 us -> 9 us
    pallas_call x1, Pallas kernels: 70.6 us -> 50.6 us  [exchange(): pl.pallas_call(exchange_kernel, out_shape=(jax.ShapeDtypeStruct((2, BLOCK...]
    pallas_call x2 -> x4, Pallas kernels: 8.49 us -> 27.4 us  [run_slots(): pl.pallas_call(functools.partial(slots_kernel, rule, places, first, last)...]
    ppermute x4 -> x3, waiting for transfers between devices: 15 us -> 0.01 us  [passed_along(): return lax.ppermute(block, axis, route)]
    ppermute x0 -> x2, waiting for transfers between devices: none -> 8.99 us  [from_diagonal(): return lax.ppermute(block, ('pos', 'tile'), route)]
    ppermute x0 -> x2, starting transfers between devices: none -> 2.58 us  [from_diagonal(): return lax.ppermute(block, ('pos', 'tile'), route)]
    ppermute x4 -> x3, starting transfers between devices: 7.98 us -> 6.01 us  [passed_along(): return lax.ppermute(block, axis, route)]
    slice x1 -> x2, local copies, waits for them, and re-layouts: 1.29 us -> 2.35 us  [the longest x1 1.28 us: shards(): lows.append(passed_along(object_field[:, rows, :], 'tile', -1))]
  transfers between devices with their start and end apart: 4 -> 5, of which waited for: 3 -> 2; matrix products, arithmetic and copies ran while one was open for 1% -> 2% of each run, Pallas kernels for 4% -> 20%
where the time goes in v2:
time: 106 us; the launch traced here: 105 us
  Pallas kernels  78 us (74%)
  waiting for transfers between devices  9 us (8%)
  starting transfers between devices  8.59 us (8%)
  local copies, waits for them, and re-layouts  8.14 us (8%)
  between operations  1.51 us (1%)
    pallas_call x1, Pallas kernels, exchange(): pl.pallas_call(exchange_kernel, out_shape=(jax.ShapeDtypeStruct((2, BLOCK...  50.6 us
    pallas_call x4, Pallas kernels, run_slots(): pl.pallas_call(functools.partial(slots_kernel, rule, places, first, last)...  27.4 us
    ppermute x2, waiting for transfers between devices, from_diagonal(): return lax.ppermute(block, ('pos', 'tile'), route)  8.99 us
    ppermute x3, starting transfers between devices, passed_along(): return lax.ppermute(block, axis, route)  6.01 us
    unnamed x20, local copies, waits for them, and re-layouts  4.34 us
    ppermute x2, starting transfers between devices, from_diagonal(): return lax.ppermute(block, ('pos', 'tile'), route)  2.58 us
  transfers between devices with their start and end apart: 5, of which 2 were waited for; matrix products, arithmetic and copies ran while one was open for 2% of the time, Pallas kernels for 20%

profile of v2, /device:TPU:1, one launch (start us, length us, event | category | flops | bytes accessed | tf_op | source)
XLA Modules:
  0.0 105.2 jit_solution(2742318789183521982)
XLA Ops:
  0.6 0.0 copy-start.7
  0.6 0.0 copy-start.5
  0.7 0.0 copy-start.8
  0.7 0.0 copy-start.6
  0.7 0.0 copy-start
  0.7 0.0 copy-start.1
  0.7 0.0 copy-start.3
  0.7 0.0 copy-start.4
  0.7 1.4 %slice.19 = f32[2,512,256]{2,1,0:T(8,128)S(1)} slice(f32[2,512,512]{2,1,0:T(8,128)} %obj_ref.1), slice={[0:2], [0:512], [0:256]} | slice | bytes 2097152 | tf_op jit(solution)/shard_map/slice | solution.py:431
  2.2 3.4 %collective-permute-start.4 = (f32[2,512,256]{2,1,0:T(8,128)S(1)}, f32[2,512,256]{2,1,0:T(8,128)S(1)}, u32[]{:S(2)}, u32[]{:S(2)}) collective-permute-start(f32[2,512,256]{2,1,0:T(8,128)S(1)} %slice.19), channel_id=1, source_target_pairs={{4,0},{8,4},{12,8},{16,12},{20,16},{24,20},{28,24},{32,28},{36,32}... | collective-permute-start | bytes 3145736 | tf_op jit(solution)/shard_map/ppermute | solution.py:261
  5.6 1.3 %fusion.1 = (f32[2,128,512]{2,1,0:T(8,128)S(1)}, f32[2,128,512]{2,1,0:T(8,128)S(1)}) fusion(f32[2,512,512]{2,1,0:T(8,128)} %obj_ref.1), kind=kLoop, calls=%fused_computation.1 | loop fusion | bytes 2097152 | tf_op jit(solution)/shard_map/slice | solution.py:429
  6.9 1.3 %collective-permute-start.2 = (f32[2,128,512]{2,1,0:T(8,128)S(1)}, f32[2,128,512]{2,1,0:T(8,128)S(1)}, u32[]{:S(2)}, u32[]{:S(2)}) collective-permute-start(f32[2,128,512]{2,1,0:T(8,128)S(1)} %get-tuple-element.32), channel_id=1, source_target_pairs={{1,0},{2,1},{3,2},{5,4},{6,5},{7,6},{9,8},{10,9},{11,10},{13,12},{... | collective-permute-start | bytes 1572872 | tf_op jit(solution)/shard_map/ppermute | solution.py:261
  8.2 1.1 %fusion = (f32[2,128,256]{2,1,0:T(8,128)S(1)}, f32[2,128,256]{2,1,0:T(8,128)S(1)}) fusion(f32[2,512,512]{2,1,0:T(8,128)} %obj_ref.1), kind=kLoop, calls=%fused_computation | loop fusion | bytes 1048576 | tf_op jit(solution)/shard_map/slice | solution.py:430
  9.3 1.3 %collective-permute-start.3 = (f32[2,128,256]{2,1,0:T(8,128)S(1)}, f32[2,128,256]{2,1,0:T(8,128)S(1)}, u32[]{:S(2)}, u32[]{:S(2)}) collective-permute-start(f32[2,128,256]{2,1,0:T(8,128)S(1)} %get-tuple-element.30), channel_id=1, source_target_pairs={{5,0},{6,1},{7,2},{9,4},{10,5},{11,6},{13,8},{14,9},{15,10},{17,12... | collective-permute-start | bytes 786440 | tf_op jit(solution)/shard_map/ppermute | solution.py:267
  10.6 1.3 %collective-permute-start = (f32[2,128,512]{2,1,0:T(8,128)S(1)}, f32[2,128,512]{2,1,0:T(8,128)S(1)}, u32[]{:S(2)}, u32[]{:S(2)}) collective-permute-start(f32[2,128,512]{2,1,0:T(8,128)S(1)} %get-tuple-element.33), channel_id=1, source_target_pairs={{1,0},{2,1},{3,2},{5,4},{6,5},{7,6},{9,8},{10,9},{11,10},{13,12},{... | collective-permute-start | bytes 1572872 | tf_op jit(solution)/shard_map/ppermute | solution.py:261
  11.9 1.3 %collective-permute-start.1 = (f32[2,128,256]{2,1,0:T(8,128)S(1)}, f32[2,128,256]{2,1,0:T(8,128)S(1)}, u32[]{:S(2)}, u32[]{:S(2)}) collective-permute-start(f32[2,128,256]{2,1,0:T(8,128)S(1)} %get-tuple-element.31), channel_id=1, source_target_pairs={{5,0},{6,1},{7,2},{9,4},{10,5},{11,6},{13,8},{14,9},{15,10},{17,12... | collective-permute-start | bytes 786440 | tf_op jit(solution)/shard_map/ppermute | solution.py:267
  13.8 0.0 copy-done.7
  13.8 0.0 copy-done.5
  13.9 0.0 copy-start.2
  13.9 2.2 %copy-done.2 = bf16[1,1,32,256,256]{4,3,2,1,0:T(8,128)(2,1)S(1)} copy-done((bf16[1,1,32,256,256]{4,3,2,1,0:T(8,128)(2,1)S(1)}, bf16[1,1,32,256,256]{4,3,2,1,0:T(8,128)(2,1)}, u32[]{:S(2)}) %copy-start.2) | copy-done | bytes 4194328
  16.1 9.0 %shard_map.113 = (f32[2,6,768,128]{3,2,1,0:T(8,128)S(1)}, f32[2,6,768,128]{3,2,1,0:T(8,128)S(1)}, f32[2,256,256]{2,1,0:T(8,128)S(1)}, f32[2,256,256]{2,1,0:T(8,128)S(1)}) custom-call(s32[1,1,32]{2,1,0:T(1,128)S(1)} %copy-done.3, s32[1,1,32]{2,1,0:T(1,128)S(1)} %copy-done.4, s32[1,1]{1,0:T(1,128)S(6)} %copy.38.count_ref, ...), custom_call_target="tpu_custom_call" | custom-call | flops 10000000000 | bytes 4000000 | tf_op jit(solution)/shard_map/pallas_call | solution.py:234
  25.0 0.0 collective-permute-done.4.refs_0_
  25.1 3.8 %shard_map.114 = (f32[2,6,768,128]{3,2,1,0:T(8,128)S(1)}, f32[2,6,768,128]{3,2,1,0:T(8,128)S(1)}, f32[2,256,256]{2,1,0:T(8,128)S(1)}, f32[2,256,256]{2,1,0:T(8,128)S(1)}) custom-call(s32[1,1,32]{2,1,0:T(1,128)S(1)} %copy-done.3, s32[1,1,32]{2,1,0:T(1,128)S(1)} %copy-done.4, ...), custom_call_target="tpu_custom_call", output_to_operand_aliasing={{0}: (9, {}), {1}: (10, {}), {2}: (11, {}), {3}: (12, {})} | custom-call | flops 10000000000 | bytes 4000000 | tf_op jit(solution)/shard_map/pallas_call | solution.py:234
  28.9 1.1 %collective-permute-done.3.refs_1_ = f32[2,128,256]{2,1,0:T(8,128)S(1)} collective-permute-done((f32[2,128,256]{2,1,0:T(8,128)S(1)}, f32[2,128,256]{2,1,0:T(8,128)S(1)}, u32[]{:S(2)}, u32[]{:S(2)}) %collective-permute-start.3) | collective-permute-done | bytes 262176 | tf_op jit(solution)/shard_map/ppermute | solution.py:267
  30.0 0.0 collective-permute-done.2.refs_0_
  30.0 8.5 %shard_map.115 = (f32[2,6,768,128]{3,2,1,0:T(8,128)S(1)}, f32[2,6,768,128]{3,2,1,0:T(8,128)S(1)}, f32[2,256,256]{2,1,0:T(8,128)S(1)}, f32[2,256,256]{2,1,0:T(8,128)S(1)}) custom-call(s32[1,1,32]{2,1,0:T(1,128)S(1)} %copy-done.3, s32[1,1,32]{2,1,0:T(1,128)S(1)} %copy-done.4, ...), custom_call_target="tpu_custom_call", output_to_operand_aliasing={{0}: (10, {}), {1}: (11, {}), {2}: (12, {}), {3}: (13, {})} | custom-call | flops 10000000000 | bytes 4000000 | tf_op jit(solution)/shard_map/pallas_call | solution.py:234
  38.4 7.9 %collective-permute-done.1.refs_1_ = f32[2,128,256]{2,1,0:T(8,128)S(1)} collective-permute-done((f32[2,128,256]{2,1,0:T(8,128)S(1)}, f32[2,128,256]{2,1,0:T(8,128)S(1)}, u32[]{:S(2)}, u32[]{:S(2)}) %collective-permute-start.1) | collective-permute-done | bytes 262176 | tf_op jit(solution)/shard_map/ppermute | solution.py:267
  46.4 0.0 collective-permute-done.refs_0_
  46.4 6.1 %shard_map.116 = (f32[2,6,768,128]{3,2,1,0:T(8,128)S(1)}, f32[2,6,768,128]{3,2,1,0:T(8,128)S(1)}, f32[2,256,256]{2,1,0:T(8,128)S(1)}, f32[2,256,256]{2,1,0:T(8,128)S(1)}) custom-call(s32[1,1,32]{2,1,0:T(1,128)S(1)} %copy-done.3, s32[1,1,32]{2,1,0:T(1,128)S(1)} %copy-done.4, ...), custom_call_target="tpu_custom_call", output_to_operand_aliasing={{0}: (10, {}), {1}: (11, {}), {2}: (12, {}), {3}: (13, {})} | custom-call | flops 10000000000 | bytes 4000000 | tf_op jit(solution)/shard_map/pallas_call | solution.py:234
  52.5 50.6 %shard_map.117 = (f32[2,512,512]{2,1,0:T(8,128)S(1)}, f32[2,256,256]{2,1,0:T(8,128)S(1)}) custom-call(f32[2,6,768,128]{3,2,1,0:T(8,128)S(1)} %get-tuple-element.28.upd_ref, f32[2,512,512]{2,1,0:T(8,128)S(1)} %copy-done, f32[512,256]{1,0:T(8,128)S(1)} %bitcast.1, f32[2,256,256]{2,1,0:T(8,128)S(1)} %copy-done.1), custom_call_target="tpu_custom_call" | custom-call | tf_op jit(solution)/shard_map/pallas_call | solution.py:397
  103.1 1.3 %copy.39 = f32[2,512,512]{2,1,0:T(8,128)} copy(f32[2,512,512]{2,1,0:T(8,128)S(1)} %get-tuple-element.36) | data formatting | bytes 4194304
  104.4 0.8 copy.40
  (6 shorter events, 0.0 us)
Async XLA Ops:
  0.6 13.2 %copy-start.7 = (bf16[2,256,256]{2,1,0:T(8,128)(2,1)S(1)}, bf16[2,256,256]{2,1,0:T(8,128)(2,1)}, u32[]{:S(2)}) copy-start(bf16[2,256,256]{2,1,0:T(8,128)(2,1)} %constant.10.clone.t3_ref) | copy-start | bytes 786436
  0.6 13.2 %copy-start.5 = (bf16[512,512]{1,0:T(8,128)(2,1)S(1)}, bf16[512,512]{1,0:T(8,128)(2,1)}, u32[]{:S(2)}) copy-start(bf16[512,512]{1,0:T(8,128)(2,1)} %constant.11.clone.t4_ref) | copy-start | bytes 1572868
  0.7 13.2 %copy-start.8 = (bf16[2,256,256]{2,1,0:T(8,128)(2,1)S(1)}, bf16[2,256,256]{2,1,0:T(8,128)(2,1)}, u32[]{:S(2)}) copy-start(bf16[2,256,256]{2,1,0:T(8,128)(2,1)} %constant.8.clone.t1_ref) | copy-start | bytes 786436
  0.7 13.2 %copy-start.6 = (bf16[512,512]{1,0:T(8,128)(2,1)S(1)}, bf16[512,512]{1,0:T(8,128)(2,1)}, u32[]{:S(2)}) copy-start(bf16[512,512]{1,0:T(8,128)(2,1)} %constant.9.clone.t2_ref) | copy-start | bytes 1572868
  0.7 13.2 %copy-start = (f32[2,512,512]{2,1,0:T(8,128)S(1)}, f32[2,512,512]{2,1,0:T(8,128)}, u32[]{:S(2)}) copy-start(f32[2,512,512]{2,1,0:T(8,128)} %obj_ref.1) | copy-start | bytes 6291460
  0.7 13.2 %copy-start.1 = (f32[2,256,256]{2,1,0:T(8,128)S(1)}, f32[2,256,256]{2,1,0:T(8,128)}, u32[]{:S(2)}) copy-start(f32[2,256,256]{2,1,0:T(8,128)} %probe_ref.1) | copy-start | bytes 1572868
  0.7 13.2 %copy-start.3 = (s32[1,1,32]{2,1,0:T(1,128)S(1)}, s32[1,1,32]{2,1,0:T(1,128)}, u32[]{:S(2)}) copy-start(s32[1,1,32]{2,1,0:T(1,128)} %rows_ref.7) | copy-start | bytes 388
  0.7 13.2 %copy-start.4 = (s32[1,1,32]{2,1,0:T(1,128)S(1)}, s32[1,1,32]{2,1,0:T(1,128)}, u32[]{:S(2)}) copy-start(s32[1,1,32]{2,1,0:T(1,128)} %cols_ref.7) | copy-start | bytes 388
  2.2 22.9 %collective-permute-start.4 = (f32[2,512,256]{2,1,0:T(8,128)S(1)}, f32[2,512,256]{2,1,0:T(8,128)S(1)}, u32[]{:S(2)}, u32[]{:S(2)}) collective-permute-start(f32[2,512,256]{2,1,0:T(8,128)S(1)} %slice.19), channel_id=1, source_target_pairs={{4,0},{8,4},{12,8},{16,12},{20,16},{24,20},{28,24},{32,28},{36,32}... | collective-permute-start | bytes 3145736 | tf_op jit(solution)/shard_map/ppermute | solution.py:261
  6.9 23.1 %collective-permute-start.2 = (f32[2,128,512]{2,1,0:T(8,128)S(1)}, f32[2,128,512]{2,1,0:T(8,128)S(1)}, u32[]{:S(2)}, u32[]{:S(2)}) collective-permute-start(f32[2,128,512]{2,1,0:T(8,128)S(1)} %get-tuple-element.32), channel_id=1, source_target_pairs={{1,0},{2,1},{3,2},{5,4},{6,5},{7,6},{9,8},{10,9},{11,10},{13,12},{... | collective-permute-start | bytes 1572872 | tf_op jit(solution)/shard_map/ppermute | solution.py:261
  9.3 20.7 %collective-permute-start.3 = (f32[2,128,256]{2,1,0:T(8,128)S(1)}, f32[2,128,256]{2,1,0:T(8,128)S(1)}, u32[]{:S(2)}, u32[]{:S(2)}) collective-permute-start(f32[2,128,256]{2,1,0:T(8,128)S(1)} %get-tuple-element.30), channel_id=1, source_target_pairs={{5,0},{6,1},{7,2},{9,4},{10,5},{11,6},{13,8},{14,9},{15,10},{17,12... | collective-permute-start | bytes 786440 | tf_op jit(solution)/shard_map/ppermute | solution.py:267
  10.6 35.8 %collective-permute-start = (f32[2,128,512]{2,1,0:T(8,128)S(1)}, f32[2,128,512]{2,1,0:T(8,128)S(1)}, u32[]{:S(2)}, u32[]{:S(2)}) collective-permute-start(f32[2,128,512]{2,1,0:T(8,128)S(1)} %get-tuple-element.33), channel_id=1, source_target_pairs={{1,0},{2,1},{3,2},{5,4},{6,5},{7,6},{9,8},{10,9},{11,10},{13,12},{... | collective-permute-start | bytes 1572872 | tf_op jit(solution)/shard_map/ppermute | solution.py:261
  11.9 34.5 %collective-permute-start.1 = (f32[2,128,256]{2,1,0:T(8,128)S(1)}, f32[2,128,256]{2,1,0:T(8,128)S(1)}, u32[]{:S(2)}, u32[]{:S(2)}) collective-permute-start(f32[2,128,256]{2,1,0:T(8,128)S(1)} %get-tuple-element.31), channel_id=1, source_target_pairs={{5,0},{6,1},{7,2},{9,4},{10,5},{11,6},{13,8},{14,9},{15,10},{17,12... | collective-permute-start | bytes 786440 | tf_op jit(solution)/shard_map/ppermute | solution.py:267
  13.9 2.2 %copy-start.2 = (bf16[1,1,32,256,256]{4,3,2,1,0:T(8,128)(2,1)S(1)}, bf16[1,1,32,256,256]{4,3,2,1,0:T(8,128)(2,1)}, u32[]{:S(2)}) copy-start(bf16[1,1,32,256,256]{4,3,2,1,0:T(8,128)(2,1)} %amp_ref.7) | copy-start | bytes 12582916

commit v3 on v2

--- a/solution.py
+++ b/solution.py
@@ -72,6 +72,17 @@
     def amp_copy(i, k=0):
         return pltpu.make_async_copy(amp_ref.at[0, 0, order[i]], amp_buf[k], amp_sem.at[k])
 
+    final = jnp.maximum(total - 1, 0)
+    pairs = (total + 1) // 2
+
+    def fetch(pair, half):
+        for m in range(2):
+            amp_copy(jnp.minimum(2 * pair + m, final), 2 * half + m).start()
+
+    @pl.when(total > 0)
+    def _():
+        fetch(0, 0)
+
     if first:
         for b in range(2):
             bring(probe_ref.at[:, :, b * H : (b + 1) * H], lanes_buf.at[:, b])
@@ -160,13 +171,6 @@
                 spot = (comp, c0 + b, pl.ds(r + q, H, stride=2), slice(None))
                 upd_ref[spot] = upd_ref[spot] + val
 
-    final = jnp.maximum(total - 1, 0)
-    pairs = (total + 1) // 2
-
-    def fetch(pair, half):
-        for m in range(2):
-            amp_copy(jnp.minimum(2 * pair + m, final), 2 * half + m).start()
-
     def work(pair, half):
         follow = jnp.minimum(pair + 1, pairs - 1)
         ids = [jnp.minimum(2 * pair + m, final) for m in range(2)]
@@ -191,7 +195,6 @@
 
     @pl.when(total > 0)
     def _():
-        fetch(0, 0)
         for m in range(2):
             for q in range(2):
                 enter(jnp.minimum(m, final), m, q)
@@ -269,14 +272,13 @@
 
 def exchange_kernel(
     upd_ref, obj_ref, sum_ref, probe_ref, out_ref, grad_ref,
-    from_left, from_above, corner, pair_in, part, x_in, piece, tile_in, gathered,
+    from_left, from_above, corner, pair_in, part, x_in, piece, z_in, y_in, gathered,
     right_send, right_recv, low_send, low_recv, pair_send, pair_recv, x_send, x_recv,
-    t_send, t_recv, tg_send, tg_recv, xg_send, xg_recv, cg_send, cg_recv,
+    z_send, z_recv, y_send, y_recv, zg_send, zg_recv, xg_send, xg_recv, cg_send, cg_recv,
 ):
     p = lax.axis_index("pos")
     t = lax.axis_index("tile")
     x, z, core = p // 8, (p // 2) % 4, p % 2
-    g = z * 4 + t
 
     def pos_of(xx, zz, cc):
         return xx * 8 + zz * 2 + cc
@@ -286,12 +288,14 @@
     below = {"pos": p, "tile": (t + 1) % 4}
     partner = {"pos": pos_of(x, z, 1 - core), "tile": t}
     x_peers = [{"pos": pos_of((x + d) % 4, z, core), "tile": t} for d in (1, 2, 3)]
-    g_peers = [{"pos": pos_of(x, ((g + d) % 16) // 4, core), "tile": (g + d) % 4} for d in range(1, 16)]
+    z_peers = [{"pos": pos_of(x, (z + d) % 4, core), "tile": t} for d in (1, 2, 3)]
+    y_peers = [{"pos": p, "tile": (t + d) % 4} for d in (1, 2, 3)]
 
     barrier = pltpu.get_barrier_semaphore()
-    for peer in [right, left, partner] + x_peers + g_peers:
+    peers = [right, left, partner] + x_peers + z_peers + y_peers
+    for peer in peers:
         pl.semaphore_signal(barrier, inc=1, device_id=peer, device_id_type=pl.DeviceIdType.MESH)
-    pl.semaphore_wait(barrier, 21)
+    pl.semaphore_wait(barrier, len(peers))
 
     started = []
 
@@ -304,7 +308,8 @@
         started.append(copy)
         return copy
 
-    low1 = send(upd_ref.at[:, 2:4, 2 * N :, :], from_above.at[:, 2:4], low_send.at[0], low_recv.at[0], below)
+    edge = send(upd_ref.at[:, 4:6, 2 * N :, :], from_left.at[:, :, 2 * N :, :], right_send.at[0], right_recv.at[0], right)
+    low1 = send(upd_ref.at[:, 2, 2 * N :, :], from_above.at[:, 2], low_send.at[0], low_recv.at[0], below)
     half = send(sum_ref.at[pl.ds((1 - core) * N, N)], pair_in, pair_send.at[0], pair_recv.at[0], partner)
     half.wait_recv()
     part[...] = sum_ref[pl.ds(core * N, N), :] + pair_in[...]
@@ -312,7 +317,6 @@
         send(part.at[pl.ds(((x + d) % 4) * 64, 64)], x_in.at[d - 1], x_send.at[d - 1], x_recv.at[d - 1], x_peers[d - 1])
         for d in (1, 2, 3)
     ]
-    edge = send(upd_ref.at[:, 4:6, 2 * N :, :], from_left.at[:, :, 2 * N :, :], right_send.at[0], right_recv.at[0], right)
     has_left = (p > 0).astype(jnp.float32)
     has_above = (t > 0).astype(jnp.float32)
     power = jnp.sum(probe_ref[...] * probe_ref[...]) * (1.0 / (N * N)) + 1e-06
@@ -324,30 +328,30 @@
     for rg in range(8):
         for lg in range(2):
             piece[rg * 2 + lg] = shard[rg * 8 : rg * 8 + 8, lg * H : (lg + 1) * H]
-    t_copies = [
-        send(piece.at[(g + d) % 16], tile_in.at[d - 1], t_send.at[d - 1], t_recv.at[d - 1], g_peers[d - 1])
-        for d in range(1, 16)
+    z_copies = [
+        send(piece.at[pl.ds(((z + d) % 4) * 4, 4)], z_in.at[d - 1], z_send.at[d - 1], z_recv.at[d - 1], z_peers[d - 1])
+        for d in (1, 2, 3)
     ]
+    low2 = send(upd_ref.at[:, 3, 2 * N :, :], from_above.at[:, 3], low_send.at[3], low_recv.at[3], below)
     mid = send(upd_ref.at[:, 4:6, N : 2 * N, :], from_left.at[:, :, N : 2 * N, :], right_send.at[1], right_recv.at[1], right)
+    for copy in z_copies:
+        copy.wait_recv()
+    y_in[t] = piece[pl.ds(z * 4, 4)] + z_in[0] + z_in[1] + z_in[2]
+    y_copies = [send(y_in.at[t], y_in.at[t], y_send.at[d - 1], y_recv.at[d - 1], y_peers[d - 1]) for d in (1, 2, 3)]
     edge.wait_recv()
     corner[...] = upd_ref[:, 0:2, 2 * N :, :] + from_left[:, :, 2 * N :, :] * has_left
-
-    for copy in t_copies:
-        copy.wait_recv()
-    own = piece[g]
-    for d in range(15):
-        own = own + tile_in[d]
-    slots = 128 * 32
-    gathered[core, x, g] = own * np.float32(1.0 / math.sqrt(slots))
-    tg_copies = [
-        send(gathered.at[core, x, g], gathered.at[core, x, g], tg_send.at[d - 1], tg_recv.at[d - 1], g_peers[d - 1])
-        for d in range(1, 16)
-    ]
     low0a = send(corner.at[:, 0], from_above.at[:, 0], low_send.at[1], low_recv.at[1], below)
     low0b = send(corner.at[:, 1], from_above.at[:, 1], low_send.at[2], low_recv.at[2], below)
+
+    for copy in y_copies:
+        copy.wait_recv()
+    slots = 128 * 32
+    mine = gathered.at[core, x, pl.ds(z * 4, 4)]
+    mine[...] = (y_in[0] + y_in[1] + y_in[2] + y_in[3]) * np.float32(1.0 / math.sqrt(slots))
+    zg_copies = [send(mine, mine, zg_send.at[d - 1], zg_recv.at[d - 1], z_peers[d - 1]) for d in (1, 2, 3)]
     top = send(upd_ref.at[:, 4:6, :N, :], from_left.at[:, :, :N, :], right_send.at[2], right_recv.at[2], right)
 
-    for copy in tg_copies:
+    for copy in zg_copies:
         copy.wait_recv()
     xg_copies = [
         send(gathered.at[core, x], gathered.at[core, x], xg_send.at[d - 1], xg_recv.at[d - 1], x_peers[d - 1])
@@ -372,6 +376,7 @@
     for b in (0, 1):
         put(b, N, upd_ref[:, b, N : 2 * N, :] + from_left[:, b, N : 2 * N, :] * has_left)
     low1.wait_recv()
+    low2.wait_recv()
     for b in (2, 3):
         put(b, 0, upd_ref[:, b, :N, :] + from_above[:, b] * has_above)
     top.wait_recv()
@@ -410,10 +415,11 @@
             pltpu.VMEM((N, N), f32),
             pltpu.VMEM((3, 64, N), f32),
             pltpu.VMEM((16, 8, H), f32),
-            pltpu.VMEM((15, 8, H), f32),
+            pltpu.VMEM((3, 4, 8, H), f32),
+            pltpu.VMEM((4, 4, 8, H), f32),
             pltpu.VMEM((2, 4, 16, 8, H), f32),
-            dma((3,)), dma((3,)), dma((3,)), dma((3,)), dma((1,)), dma((1,)), dma((3,)), dma((3,)),
-            dma((15,)), dma((15,)), dma((15,)), dma((15,)), dma((3,)), dma((3,)), dma((4,)), dma((4,)),
+            dma((3,)), dma((3,)), dma((4,)), dma((4,)), dma((1,)), dma((1,)), dma((3,)), dma((3,)),
+            *[dma((3,))] * 8, dma((4,)), dma((4,)),
         ],
         compiler_params=pltpu.CompilerParams(
             collective_id=0, has_side_effects=True, vmem_limit_bytes=32 * 1024 * 1024
@@ -423,22 +429,20 @@
 
 def shards(object_field, probe, amplitudes, corner_rows, corner_cols, counts):
     tables = [jnp.asarray(t) for t in stage_tables()]
-    lows, corners = [], []
-    for q in range(2):
-        rows = slice(q * H, (q + 1) * H)
-        lows.append(passed_along(object_field[:, rows, :], "tile", -1))
-        corners.append(from_diagonal(object_field[:, rows, :N]))
     right = passed_along(object_field[:, :, :N], "pos", -1)
+    low = passed_along(object_field[:, :N, :], "tile", -1)
+    corner = from_diagonal(object_field[:, :N, :N])
+    amplitudes = pltpu.with_memory_space_constraint(amplitudes, pltpu.HBM)
     fixed = ((corner_rows, corner_cols, counts), amplitudes, tables)
     reach = BLOCK - N
     state = run_slots(
         lambda r, c: (r <= reach) & (c <= reach), ((0, 0),), (object_field,), (probe,), False, *fixed
     )
     state = run_slots(lambda r, c: (r <= reach) & (c > reach), ((0, BLOCK),), (right,), state, False, *fixed)
-    for q, rule in enumerate((lambda r, c: (r > reach) & (r <= reach + H), lambda r, c: r > reach + H)):
-        row = BLOCK + q * H
-        state = run_slots(rule, ((row, 0), (row, BLOCK)), (lows[q], corners[q]), state, q == 1, *fixed)
-    _, update, total, _ = state
+    state = run_slots(lambda r, c: (r > reach) & (c <= reach), ((BLOCK, 0),), (low,), state, False, *fixed)
+    _, update, total, _ = run_slots(
+        lambda r, c: (r > reach) & (c > reach), ((BLOCK, BLOCK),), (corner,), state, True, *fixed
+    )
     return exchange(update, object_field, total.reshape(2 * N, N), probe)
 
 

time: 106 us -> 103 us (0.972)
  waiting for transfers between devices: 9 us -> 22.7 us
  Pallas kernels: 78 us -> 66.2 us
  starting transfers between devices: 8.59 us -> 6.01 us
  local copies, waits for them, and re-layouts: 8.14 us -> 5.99 us
    ppermute x3 -> x2, waiting for transfers between devices: 0.01 us -> 19.7 us  [passed_along(): return lax.ppermute(block, axis, route)]
    pallas_call x4, Pallas kernels: 27.4 us -> 16.4 us  [run_slots(): pl.pallas_call(functools.partial(slots_kernel, rule, places, first, last)...]
    ppermute x2 -> x1, waiting for transfers between devices: 8.99 us -> 2.98 us  [from_diagonal(): return lax.ppermute(block, ('pos', 'tile'), route)]
    unnamed x20 -> x18, local copies, waits for them, and re-layouts: 4.34 us -> 2.16 us
    ppermute x3 -> x2, starting transfers between devices: 6.01 us -> 4.71 us  [passed_along(): return lax.ppermute(block, axis, route)]
    ppermute x2 -> x1, starting transfers between devices: 2.58 us -> 1.29 us  [from_diagonal(): return lax.ppermute(block, ('pos', 'tile'), route)]
  transfers between devices with their start and end apart: 5 -> 3, of which waited for: 2 -> 3; matrix products, arithmetic and copies ran while one was open for 2% -> 2% of each run, Pallas kernels for 20% -> 12%
where the time goes in v3:
time: 103 us; the launch traced here: 102 us
  Pallas kernels  66.2 us (64%)
  waiting for transfers between devices  22.7 us (22%)
  starting transfers between devices  6.01 us (6%)
  local copies, waits for them, and re-layouts  5.99 us (6%)
  between operations  1.48 us (1%)
    pallas_call x1, Pallas kernels, exchange(): pl.pallas_call(exchange_kernel, out_shape=(jax.ShapeDtypeStruct((2, BLOCK...  49.9 us
    ppermute x2, waiting for transfers between devices, passed_along(): return lax.ppermute(block, axis, route)  19.7 us
    pallas_call x4, Pallas kernels, run_slots(): pl.pallas_call(functools.partial(slots_kernel, rule, places, first, last)...  16.4 us
    ppermute x2, starting transfers between devices, passed_along(): return lax.ppermute(block, axis, route)  4.71 us
    ppermute x1, waiting for transfers between devices, from_diagonal(): return lax.ppermute(block, ('pos', 'tile'), route)  2.98 us
    unnamed x18, local copies, waits for them, and re-layouts  2.16 us
  transfers between devices with their start and end apart: 3, of which 3 were waited for; matrix products, arithmetic and copies ran while one was open for 2% of the time, Pallas kernels for 12%

profile of v3, /device:TPU:1, one launch (start us, length us, event | category | flops | bytes accessed | tf_op | source)
XLA Modules:
  0.0 102.4 jit_solution(5336628118555814300)
XLA Ops:
  0.6 0.0 copy-start.6
  0.6 0.0 copy-start.4
  0.7 0.0 copy-start.7
  0.7 0.0 copy-start.5
  0.7 0.0 copy-start
  0.7 0.0 copy-start.1
  0.7 0.0 copy-start.2
  0.7 0.0 copy-start.3
  0.7 1.4 %slice.11 = f32[2,512,256]{2,1,0:T(8,128)S(1)} slice(f32[2,512,512]{2,1,0:T(8,128)} %obj_ref.1), slice={[0:2], [0:512], [0:256]} | slice | bytes 2097152 | tf_op jit(solution)/shard_map/slice | solution.py:432
  2.2 3.4 %collective-permute-start.2 = (f32[2,512,256]{2,1,0:T(8,128)S(1)}, f32[2,512,256]{2,1,0:T(8,128)S(1)}, u32[]{:S(2)}, u32[]{:S(2)}) collective-permute-start(f32[2,512,256]{2,1,0:T(8,128)S(1)} %slice.11), channel_id=1, source_target_pairs={{4,0},{8,4},{12,8},{16,12},{20,16},{24,20},{28,24},{32,28},{36,32}... | collective-permute-start | bytes 3145736 | tf_op jit(solution)/shard_map/ppermute | solution.py:264
  5.6 1.3 %slice.10 = f32[2,256,512]{2,1,0:T(8,128)S(1)} slice(f32[2,512,512]{2,1,0:T(8,128)} %obj_ref.1), slice={[0:2], [0:256], [0:512]} | slice | bytes 2097152 | tf_op jit(solution)/shard_map/slice | solution.py:433
  6.9 1.3 %collective-permute-start.1 = (f32[2,256,512]{2,1,0:T(8,128)S(1)}, f32[2,256,512]{2,1,0:T(8,128)S(1)}, u32[]{:S(2)}, u32[]{:S(2)}) collective-permute-start(f32[2,256,512]{2,1,0:T(8,128)S(1)} %slice.10), channel_id=1, source_target_pairs={{1,0},{2,1},{3,2},{5,4},{6,5},{7,6},{9,8},{10,9},{11,10},{13,12},{... | collective-permute-start | bytes 3145736 | tf_op jit(solution)/shard_map/ppermute | solution.py:264
  8.2 1.1 %slice.9 = f32[2,256,256]{2,1,0:T(8,128)S(1)} slice(f32[2,512,512]{2,1,0:T(8,128)} %obj_ref.1), slice={[0:2], [0:256], [0:256]} | slice | bytes 1048576 | tf_op jit(solution)/shard_map/slice | solution.py:434
  9.3 1.3 %collective-permute-start = (f32[2,256,256]{2,1,0:T(8,128)S(1)}, f32[2,256,256]{2,1,0:T(8,128)S(1)}, u32[]{:S(2)}, u32[]{:S(2)}) collective-permute-start(f32[2,256,256]{2,1,0:T(8,128)S(1)} %slice.9), channel_id=1, source_target_pairs={{5,0},{6,1},{7,2},{9,4},{10,5},{11,6},{13,8},{14,9},{15,10},{17,12... | collective-permute-start | bytes 1572872 | tf_op jit(solution)/shard_map/ppermute | solution.py:270
  11.2 0.0 copy-done.6
  11.3 0.0 copy-done.4
  11.3 0.0 copy-done.7
  11.3 0.0 copy-done.5
  11.3 0.0 copy-done
  11.3 0.0 copy-done.1
  11.3 0.0 copy-done.2
  11.3 0.0 copy-done.3
  11.3 4.3 %shard_map.113 = (f32[2,6,768,128]{3,2,1,0:T(8,128)S(1)}, f32[2,6,768,128]{3,2,1,0:T(8,128)S(1)}, f32[2,256,256]{2,1,0:T(8,128)S(1)}, f32[2,256,256]{2,1,0:T(8,128)S(1)}) custom-call(s32[1,1,32]{2,1,0:T(1,128)S(1)} %copy-done.2, s32[1,1,32]{2,1,0:T(1,128)S(1)} %copy-done.3, s32[1,1]{1,0:T(1,128)S(6)} %copy.38.count_ref, ...), custom_call_target="tpu_custom_call" | custom-call | flops 10000000000 | bytes 4000000 | tf_op jit(solution)/shard_map/pallas_call | solution.py:237
  15.6 4.4 %collective-permute-done.2.refs_0_ = f32[2,512,256]{2,1,0:T(8,128)S(1)} collective-permute-done((f32[2,512,256]{2,1,0:T(8,128)S(1)}, f32[2,512,256]{2,1,0:T(8,128)S(1)}, u32[]{:S(2)}, u32[]{:S(2)}) %collective-permute-start.2) | collective-permute-done | bytes 1048608 | tf_op jit(solution)/shard_map/ppermute | solution.py:264
  20.0 3.9 %shard_map.114 = (f32[2,6,768,128]{3,2,1,0:T(8,128)S(1)}, f32[2,6,768,128]{3,2,1,0:T(8,128)S(1)}, f32[2,256,256]{2,1,0:T(8,128)S(1)}, f32[2,256,256]{2,1,0:T(8,128)S(1)}) custom-call(s32[1,1,32]{2,1,0:T(1,128)S(1)} %copy-done.2, s32[1,1,32]{2,1,0:T(1,128)S(1)} %copy-done.3, ...), custom_call_target="tpu_custom_call", output_to_operand_aliasing={{0}: (9, {}), {1}: (10, {}), {2}: (11, {}), {3}: (12, {})} | custom-call | flops 10000000000 | bytes 4000000 | tf_op jit(solution)/shard_map/pallas_call | solution.py:237
  23.9 15.4 %collective-permute-done.1.refs_0_ = f32[2,256,512]{2,1,0:T(8,128)S(1)} collective-permute-done((f32[2,256,512]{2,1,0:T(8,128)S(1)}, f32[2,256,512]{2,1,0:T(8,128)S(1)}, u32[]{:S(2)}, u32[]{:S(2)}) %collective-permute-start.1) | collective-permute-done | bytes 1048608 | tf_op jit(solution)/shard_map/ppermute | solution.py:264
  39.3 4.1 %shard_map.115 = (f32[2,6,768,128]{3,2,1,0:T(8,128)S(1)}, f32[2,6,768,128]{3,2,1,0:T(8,128)S(1)}, f32[2,256,256]{2,1,0:T(8,128)S(1)}, f32[2,256,256]{2,1,0:T(8,128)S(1)}) custom-call(s32[1,1,32]{2,1,0:T(1,128)S(1)} %copy-done.2, s32[1,1,32]{2,1,0:T(1,128)S(1)} %copy-done.3, ...), custom_call_target="tpu_custom_call", output_to_operand_aliasing={{0}: (9, {}), {1}: (10, {}), {2}: (11, {}), {3}: (12, {})} | custom-call | flops 10000000000 | bytes 4000000 | tf_op jit(solution)/shard_map/pallas_call | solution.py:237
  43.4 3.0 %collective-permute-done.refs_0_ = f32[2,256,256]{2,1,0:T(8,128)S(1)} collective-permute-done((f32[2,256,256]{2,1,0:T(8,128)S(1)}, f32[2,256,256]{2,1,0:T(8,128)S(1)}, u32[]{:S(2)}, u32[]{:S(2)}) %collective-permute-start) | collective-permute-done | bytes 524320 | tf_op jit(solution)/shard_map/ppermute | solution.py:270
  46.4 4.1 %shard_map.116 = (f32[2,6,768,128]{3,2,1,0:T(8,128)S(1)}, f32[2,6,768,128]{3,2,1,0:T(8,128)S(1)}, f32[2,256,256]{2,1,0:T(8,128)S(1)}, f32[2,256,256]{2,1,0:T(8,128)S(1)}) custom-call(s32[1,1,32]{2,1,0:T(1,128)S(1)} %copy-done.2, s32[1,1,32]{2,1,0:T(1,128)S(1)} %copy-done.3, ...), custom_call_target="tpu_custom_call", output_to_operand_aliasing={{0}: (9, {}), {1}: (10, {}), {2}: (11, {}), {3}: (12, {})} | custom-call | flops 10000000000 | bytes 4000000 | tf_op jit(solution)/shard_map/pallas_call | solution.py:237
  50.4 49.9 %shard_map.117 = (f32[2,512,512]{2,1,0:T(8,128)S(1)}, f32[2,256,256]{2,1,0:T(8,128)S(1)}) custom-call(f32[2,6,768,128]{3,2,1,0:T(8,128)S(1)} %get-tuple-element.28.upd_ref, f32[2,512,512]{2,1,0:T(8,128)S(1)} %copy-done, f32[512,256]{1,0:T(8,128)S(1)} %bitcast.1, f32[2,256,256]{2,1,0:T(8,128)S(1)} %copy-done.1), custom_call_target="tpu_custom_call" | custom-call | tf_op jit(solution)/shard_map/pallas_call | solution.py:402
  100.3 1.3 %copy.39 = f32[2,512,512]{2,1,0:T(8,128)} copy(f32[2,512,512]{2,1,0:T(8,128)S(1)} %get-tuple-element.32) | data formatting | bytes 4194304
  101.6 0.8 copy.40
Async XLA Ops:
  0.6 10.6 %copy-start.6 = (bf16[2,256,256]{2,1,0:T(8,128)(2,1)S(1)}, bf16[2,256,256]{2,1,0:T(8,128)(2,1)}, u32[]{:S(2)}) copy-start(bf16[2,256,256]{2,1,0:T(8,128)(2,1)} %constant.10.clone.t3_ref) | copy-start | bytes 786436
  0.6 10.6 %copy-start.4 = (bf16[512,512]{1,0:T(8,128)(2,1)S(1)}, bf16[512,512]{1,0:T(8,128)(2,1)}, u32[]{:S(2)}) copy-start(bf16[512,512]{1,0:T(8,128)(2,1)} %constant.11.clone.t4_ref) | copy-start | bytes 1572868
  0.7 10.6 %copy-start.7 = (bf16[2,256,256]{2,1,0:T(8,128)(2,1)S(1)}, bf16[2,256,256]{2,1,0:T(8,128)(2,1)}, u32[]{:S(2)}) copy-start(bf16[2,256,256]{2,1,0:T(8,128)(2,1)} %constant.8.clone.t1_ref) | copy-start | bytes 786436
  0.7 10.6 %copy-start.5 = (bf16[512,512]{1,0:T(8,128)(2,1)S(1)}, bf16[512,512]{1,0:T(8,128)(2,1)}, u32[]{:S(2)}) copy-start(bf16[512,512]{1,0:T(8,128)(2,1)} %constant.9.clone.t2_ref) | copy-start | bytes 1572868
  0.7 10.6 %copy-start = (f32[2,512,512]{2,1,0:T(8,128)S(1)}, f32[2,512,512]{2,1,0:T(8,128)}, u32[]{:S(2)}) copy-start(f32[2,512,512]{2,1,0:T(8,128)} %obj_ref.1) | copy-start | bytes 6291460
  0.7 10.6 %copy-start.1 = (f32[2,256,256]{2,1,0:T(8,128)S(1)}, f32[2,256,256]{2,1,0:T(8,128)}, u32[]{:S(2)}) copy-start(f32[2,256,256]{2,1,0:T(8,128)} %probe_ref.1) | copy-start | bytes 1572868
  0.7 10.6 %copy-start.2 = (s32[1,1,32]{2,1,0:T(1,128)S(1)}, s32[1,1,32]{2,1,0:T(1,128)}, u32[]{:S(2)}) copy-start(s32[1,1,32]{2,1,0:T(1,128)} %rows_ref.7) | copy-start | bytes 388
  0.7 10.6 %copy-start.3 = (s32[1,1,32]{2,1,0:T(1,128)S(1)}, s32[1,1,32]{2,1,0:T(1,128)}, u32[]{:S(2)}) copy-start(s32[1,1,32]{2,1,0:T(1,128)} %cols_ref.7) | copy-start | bytes 388
  2.2 17.8 %collective-permute-start.2 = (f32[2,512,256]{2,1,0:T(8,128)S(1)}, f32[2,512,256]{2,1,0:T(8,128)S(1)}, u32[]{:S(2)}, u32[]{:S(2)}) collective-permute-start(f32[2,512,256]{2,1,0:T(8,128)S(1)} %slice.11), channel_id=1, source_target_pairs={{4,0},{8,4},{12,8},{16,12},{20,16},{24,20},{28,24},{32,28},{36,32}... | collective-permute-start | bytes 3145736 | tf_op jit(solution)/shard_map/ppermute | solution.py:264
  6.9 32.4 %collective-permute-start.1 = (f32[2,256,512]{2,1,0:T(8,128)S(1)}, f32[2,256,512]{2,1,0:T(8,128)S(1)}, u32[]{:S(2)}, u32[]{:S(2)}) collective-permute-start(f32[2,256,512]{2,1,0:T(8,128)S(1)} %slice.10), channel_id=1, source_target_pairs={{1,0},{2,1},{3,2},{5,4},{6,5},{7,6},{9,8},{10,9},{11,10},{13,12},{... | collective-permute-start | bytes 3145736 | tf_op jit(solution)/shard_map/ppermute | solution.py:264
  9.3 37.1 %collective-permute-start = (f32[2,256,256]{2,1,0:T(8,128)S(1)}, f32[2,256,256]{2,1,0:T(8,128)S(1)}, u32[]{:S(2)}, u32[]{:S(2)}) collective-permute-start(f32[2,256,256]{2,1,0:T(8,128)S(1)} %slice.9), channel_id=1, source_target_pairs={{5,0},{6,1},{7,2},{9,4},{10,5},{11,6},{13,8},{14,9},{15,10},{17,12... | collective-permute-start | bytes 1572872 | tf_op jit(solution)/shard_map/ppermute | solution.py:270

commit v4 on v3

--- a/solution.py
+++ b/solution.py
@@ -297,19 +297,37 @@
         pl.semaphore_signal(barrier, inc=1, device_id=peer, device_id_type=pl.DeviceIdType.MESH)
     pl.semaphore_wait(barrier, len(peers))
 
-    started = []
-
-    def send(source, target, send_sem, recv_sem, peer):
-        copy = pltpu.make_async_remote_copy(
+    started, rims = [], []
+    sends_right, sends_low, has_left, has_above = p < 31, t < 3, p > 0, t > 0
+
+    def describe(source, target, send_sem, recv_sem, peer):
+        return pltpu.make_async_remote_copy(
             src_ref=source, dst_ref=target, send_sem=send_sem, recv_sem=recv_sem,
             device_id=peer, device_id_type=pl.DeviceIdType.MESH,
         )
+
+    def send(*where):
+        copy = describe(*where)
         copy.start()
         started.append(copy)
         return copy
 
-    edge = send(upd_ref.at[:, 4:6, 2 * N :, :], from_left.at[:, :, 2 * N :, :], right_send.at[0], right_recv.at[0], right)
-    low1 = send(upd_ref.at[:, 2, 2 * N :, :], from_above.at[:, 2], low_send.at[0], low_recv.at[0], below)
+    def send_rim(go, *where):
+        copy = describe(*where)
+        pl.when(go)(copy.start)
+        rims.append((go, copy))
+        return copy
+
+    @pl.when(p == 0)
+    def _():
+        from_left[...] = jnp.zeros_like(from_left)
+
+    @pl.when(t == 0)
+    def _():
+        from_above[...] = jnp.zeros_like(from_above)
+
+    edge = send_rim(sends_right, upd_ref.at[:, 4:6, 2 * N :, :], from_left.at[:, :, 2 * N :, :], right_send.at[0], right_recv.at[0], right)
+    low1 = send_rim(sends_low, upd_ref.at[:, 2, 2 * N :, :], from_above.at[:, 2], low_send.at[0], low_recv.at[0], below)
     half = send(sum_ref.at[pl.ds((1 - core) * N, N)], pair_in, pair_send.at[0], pair_recv.at[0], partner)
     half.wait_recv()
     part[...] = sum_ref[pl.ds(core * N, N), :] + pair_in[...]
@@ -317,8 +335,6 @@
         send(part.at[pl.ds(((x + d) % 4) * 64, 64)], x_in.at[d - 1], x_send.at[d - 1], x_recv.at[d - 1], x_peers[d - 1])
         for d in (1, 2, 3)
     ]
-    has_left = (p > 0).astype(jnp.float32)
-    has_above = (t > 0).astype(jnp.float32)
     power = jnp.sum(probe_ref[...] * probe_ref[...]) * (1.0 / (N * N)) + 1e-06
     scale = 1.0 / jnp.full((1, H), power, jnp.float32)
 
@@ -332,16 +348,16 @@
         send(piece.at[pl.ds(((z + d) % 4) * 4, 4)], z_in.at[d - 1], z_send.at[d - 1], z_recv.at[d - 1], z_peers[d - 1])
         for d in (1, 2, 3)
     ]
-    low2 = send(upd_ref.at[:, 3, 2 * N :, :], from_above.at[:, 3], low_send.at[3], low_recv.at[3], below)
-    mid = send(upd_ref.at[:, 4:6, N : 2 * N, :], from_left.at[:, :, N : 2 * N, :], right_send.at[1], right_recv.at[1], right)
+    low2 = send_rim(sends_low, upd_ref.at[:, 3, 2 * N :, :], from_above.at[:, 3], low_send.at[3], low_recv.at[3], below)
+    mid = send_rim(sends_right, upd_ref.at[:, 4:6, N : 2 * N, :], from_left.at[:, :, N : 2 * N, :], right_send.at[1], right_recv.at[1], right)
     for copy in z_copies:
         copy.wait_recv()
     y_in[t] = piece[pl.ds(z * 4, 4)] + z_in[0] + z_in[1] + z_in[2]
     y_copies = [send(y_in.at[t], y_in.at[t], y_send.at[d - 1], y_recv.at[d - 1], y_peers[d - 1]) for d in (1, 2, 3)]
-    edge.wait_recv()
-    corner[...] = upd_ref[:, 0:2, 2 * N :, :] + from_left[:, :, 2 * N :, :] * has_left
-    low0a = send(corner.at[:, 0], from_above.at[:, 0], low_send.at[1], low_recv.at[1], below)
-    low0b = send(corner.at[:, 1], from_above.at[:, 1], low_send.at[2], low_recv.at[2], below)
+    pl.when(has_left)(edge.wait_recv)
+    corner[...] = upd_ref[:, 0:2, 2 * N :, :] + from_left[:, :, 2 * N :, :]
+    low0a = send_rim(sends_low, corner.at[:, 0], from_above.at[:, 0], low_send.at[1], low_recv.at[1], below)
+    low0b = send_rim(sends_low, corner.at[:, 1], from_above.at[:, 1], low_send.at[2], low_recv.at[2], below)
 
     for copy in y_copies:
         copy.wait_recv()
@@ -349,7 +365,7 @@
     mine = gathered.at[core, x, pl.ds(z * 4, 4)]
     mine[...] = (y_in[0] + y_in[1] + y_in[2] + y_in[3]) * np.float32(1.0 / math.sqrt(slots))
     zg_copies = [send(mine, mine, zg_send.at[d - 1], zg_recv.at[d - 1], z_peers[d - 1]) for d in (1, 2, 3)]
-    top = send(upd_ref.at[:, 4:6, :N, :], from_left.at[:, :, :N, :], right_send.at[2], right_recv.at[2], right)
+    top = send_rim(sends_right, upd_ref.at[:, 4:6, :N, :], from_left.at[:, :, :N, :], right_send.at[2], right_recv.at[2], right)
 
     for copy in zg_copies:
         copy.wait_recv()
@@ -372,14 +388,14 @@
         cg_copies.append(
             send(gathered.at[core, came], gathered.at[core, came], cg_send.at[d], cg_recv.at[d], partner)
         )
-    mid.wait_recv()
+    pl.when(has_left)(mid.wait_recv)
     for b in (0, 1):
-        put(b, N, upd_ref[:, b, N : 2 * N, :] + from_left[:, b, N : 2 * N, :] * has_left)
-    low1.wait_recv()
-    low2.wait_recv()
+        put(b, N, upd_ref[:, b, N : 2 * N, :] + from_left[:, b, N : 2 * N, :])
+    pl.when(has_above)(low1.wait_recv)
+    pl.when(has_above)(low2.wait_recv)
     for b in (2, 3):
-        put(b, 0, upd_ref[:, b, :N, :] + from_above[:, b] * has_above)
-    top.wait_recv()
+        put(b, 0, upd_ref[:, b, :N, :] + from_above[:, b])
+    pl.when(has_left)(top.wait_recv)
     for copy in cg_copies:
         copy.wait_recv()
     for h in range(2):
@@ -387,12 +403,14 @@
             for rg in range(8):
                 for lg in range(2):
                     grad_ref[h, xx * 64 + rg * 8 : xx * 64 + rg * 8 + 8, lg * H : (lg + 1) * H] = gathered[h, xx, rg * 2 + lg]
-    low0a.wait_recv()
-    low0b.wait_recv()
+    pl.when(has_above)(low0a.wait_recv)
+    pl.when(has_above)(low0b.wait_recv)
     for b in (0, 1):
-        put(b, 0, upd_ref[:, b, :N, :] + from_left[:, b, :N, :] * has_left + from_above[:, b] * has_above)
+        put(b, 0, upd_ref[:, b, :N, :] + from_left[:, b, :N, :] + from_above[:, b])
     for copy in started:
         copy.wait_send()
+    for go, copy in rims:
+        pl.when(go)(copy.wait_send)
 
 
 def exchange(update, object_field, total, probe):
@@ -429,20 +447,23 @@
 
 def shards(object_field, probe, amplitudes, corner_rows, corner_cols, counts):
     tables = [jnp.asarray(t) for t in stage_tables()]
+    amplitudes = pltpu.with_memory_space_constraint(amplitudes, pltpu.HBM)
+    lows, corners = [], []
+    for q in range(2):
+        rows = slice(q * H, (q + 1) * H)
+        lows.append(passed_along(object_field[:, rows, :], "tile", -1))
+        corners.append(from_diagonal(object_field[:, rows, :N]))
     right = passed_along(object_field[:, :, :N], "pos", -1)
-    low = passed_along(object_field[:, :N, :], "tile", -1)
-    corner = from_diagonal(object_field[:, :N, :N])
-    amplitudes = pltpu.with_memory_space_constraint(amplitudes, pltpu.HBM)
     fixed = ((corner_rows, corner_cols, counts), amplitudes, tables)
     reach = BLOCK - N
     state = run_slots(
         lambda r, c: (r <= reach) & (c <= reach), ((0, 0),), (object_field,), (probe,), False, *fixed
     )
     state = run_slots(lambda r, c: (r <= reach) & (c > reach), ((0, BLOCK),), (right,), state, False, *fixed)
-    state = run_slots(lambda r, c: (r > reach) & (c <= reach), ((BLOCK, 0),), (low,), state, False, *fixed)
-    _, update, total, _ = run_slots(
-        lambda r, c: (r > reach) & (c > reach), ((BLOCK, BLOCK),), (corner,), state, True, *fixed
-    )
+    for q, rule in enumerate((lambda r, c: (r > reach) & (r <= reach + H), lambda r, c: r > reach + H)):
+        row = BLOCK + q * H
+        state = run_slots(rule, ((row, 0), (row, BLOCK)), (lows[q], corners[q]), state, q == 1, *fixed)
+    _, update, total, _ = state
     return exchange(update, object_field, total.reshape(2 * N, N), probe)
 
 

time: 103 us -> 96.8 us (0.940)
  waiting for transfers between devices: 22.7 us -> 13 us
  starting transfers between devices: 6.01 us -> 8.59 us
    ppermute x2 -> x3, waiting for transfers between devices: 19.7 us -> 0.01 us  [passed_along(): return lax.ppermute(block, axis, route)]
    ppermute x1 -> x2, waiting for transfers between devices: 2.98 us -> 12.9 us  [from_diagonal(): return lax.ppermute(block, ('pos', 'tile'), route)]
    pallas_call x4, Pallas kernels: 16.4 us -> 25.2 us  [run_slots(): pl.pallas_call(functools.partial(slots_kernel, rule, places, first, last)...]
    pallas_call x1, Pallas kernels: 49.9 us -> 41.7 us  [exchange(): pl.pallas_call(exchange_kernel, out_shape=(jax.ShapeDtypeStruct((2, BLOCK...]
    ppermute x2 -> x3, starting transfers between devices: 4.71 us -> 6.01 us  [passed_along(): return lax.ppermute(block, axis, route)]
    ppermute x1 -> x2, starting transfers between devices: 1.29 us -> 2.58 us  [from_diagonal(): return lax.ppermute(block, ('pos', 'tile'), route)]
  transfers between devices with their start and end apart: 3 -> 5, of which waited for: 3 -> 2; matrix products, arithmetic and copies ran while one was open for 2% -> 2% of each run, Pallas kernels for 12% -> 20%
where the time goes in v4:
time: 96.8 us; the launch traced here: 95.9 us
  Pallas kernels  66.9 us (69%)
  waiting for transfers between devices  13 us (13%)
  starting transfers between devices  8.59 us (9%)
  local copies, waits for them, and re-layouts  5.96 us (6%)
  between operations  1.5 us (2%)
    pallas_call x1, Pallas kernels, exchange(): pl.pallas_call(exchange_kernel, out_shape=(jax.ShapeDtypeStruct((2, BLOCK...  41.7 us
    pallas_call x4, Pallas kernels, run_slots(): pl.pallas_call(functools.partial(slots_kernel, rule, places, first, last)...  25.2 us
    ppermute x2, waiting for transfers between devices, from_diagonal(): return lax.ppermute(block, ('pos', 'tile'), route)  12.9 us
    ppermute x3, starting transfers between devices, passed_along(): return lax.ppermute(block, axis, route)  6.01 us
    ppermute x2, starting transfers between devices, from_diagonal(): return lax.ppermute(block, ('pos', 'tile'), route)  2.58 us
    unnamed x18, local copies, waits for them, and re-layouts  2.16 us
  transfers between devices with their start and end apart: 5, of which 2 were waited for; matrix products, arithmetic and copies ran while one was open for 2% of the time, Pallas kernels for 20%

profile of v4, /device:TPU:1, one launch (start us, length us, event | category | flops | bytes accessed | tf_op | source)
XLA Modules:
  0.0 95.9 jit_solution(9803169517797188778)
XLA Ops:
  0.6 0.0 copy-start.6
  0.6 0.0 copy-start.4
  0.7 0.0 copy-start.7
  0.7 0.0 copy-start.5
  0.7 0.0 copy-start
  0.7 0.0 copy-start.1
  0.7 0.0 copy-start.2
  0.7 0.0 copy-start.3
  0.7 1.4 %slice.19 = f32[2,512,256]{2,1,0:T(8,128)S(1)} slice(f32[2,512,512]{2,1,0:T(8,128)} %obj_ref.1), slice={[0:2], [0:512], [0:256]} | slice | bytes 2097152 | tf_op jit(solution)/shard_map/slice | solution.py:456
  2.2 3.4 %collective-permute-start.4 = (f32[2,512,256]{2,1,0:T(8,128)S(1)}, f32[2,512,256]{2,1,0:T(8,128)S(1)}, u32[]{:S(2)}, u32[]{:S(2)}) collective-permute-start(f32[2,512,256]{2,1,0:T(8,128)S(1)} %slice.19), channel_id=1, source_target_pairs={{4,0},{8,4},{12,8},{16,12},{20,16},{24,20},{28,24},{32,28},{36,32}... | collective-permute-start | bytes 3145736 | tf_op jit(solution)/shard_map/ppermute | solution.py:264
  5.6 1.3 %fusion.1 = (f32[2,128,512]{2,1,0:T(8,128)S(1)}, f32[2,128,512]{2,1,0:T(8,128)S(1)}) fusion(f32[2,512,512]{2,1,0:T(8,128)} %obj_ref.1), kind=kLoop, calls=%fused_computation.1 | loop fusion | bytes 2097152 | tf_op jit(solution)/shard_map/slice | solution.py:454
  6.9 1.3 %collective-permute-start.2 = (f32[2,128,512]{2,1,0:T(8,128)S(1)}, f32[2,128,512]{2,1,0:T(8,128)S(1)}, u32[]{:S(2)}, u32[]{:S(2)}) collective-permute-start(f32[2,128,512]{2,1,0:T(8,128)S(1)} %get-tuple-element.32), channel_id=1, source_target_pairs={{1,0},{2,1},{3,2},{5,4},{6,5},{7,6},{9,8},{10,9},{11,10},{13,12},{... | collective-permute-start | bytes 1572872 | tf_op jit(solution)/shard_map/ppermute | solution.py:264
  8.2 1.1 %fusion = (f32[2,128,256]{2,1,0:T(8,128)S(1)}, f32[2,128,256]{2,1,0:T(8,128)S(1)}) fusion(f32[2,512,512]{2,1,0:T(8,128)} %obj_ref.1), kind=kLoop, calls=%fused_computation | loop fusion | bytes 1048576 | tf_op jit(solution)/shard_map/slice | solution.py:455
  9.3 1.3 %collective-permute-start.3 = (f32[2,128,256]{2,1,0:T(8,128)S(1)}, f32[2,128,256]{2,1,0:T(8,128)S(1)}, u32[]{:S(2)}, u32[]{:S(2)}) collective-permute-start(f32[2,128,256]{2,1,0:T(8,128)S(1)} %get-tuple-element.30), channel_id=1, source_target_pairs={{5,0},{6,1},{7,2},{9,4},{10,5},{11,6},{13,8},{14,9},{15,10},{17,12... | collective-permute-start | bytes 786440 | tf_op jit(solution)/shard_map/ppermute | solution.py:270
  10.6 1.3 %collective-permute-start = (f32[2,128,512]{2,1,0:T(8,128)S(1)}, f32[2,128,512]{2,1,0:T(8,128)S(1)}, u32[]{:S(2)}, u32[]{:S(2)}) collective-permute-start(f32[2,128,512]{2,1,0:T(8,128)S(1)} %get-tuple-element.33), channel_id=1, source_target_pairs={{1,0},{2,1},{3,2},{5,4},{6,5},{7,6},{9,8},{10,9},{11,10},{13,12},{... | collective-permute-start | bytes 1572872 | tf_op jit(solution)/shard_map/ppermute | solution.py:264
  11.9 1.3 %collective-permute-start.1 = (f32[2,128,256]{2,1,0:T(8,128)S(1)}, f32[2,128,256]{2,1,0:T(8,128)S(1)}, u32[]{:S(2)}, u32[]{:S(2)}) collective-permute-start(f32[2,128,256]{2,1,0:T(8,128)S(1)} %get-tuple-element.31), channel_id=1, source_target_pairs={{5,0},{6,1},{7,2},{9,4},{10,5},{11,6},{13,8},{14,9},{15,10},{17,12... | collective-permute-start | bytes 786440 | tf_op jit(solution)/shard_map/ppermute | solution.py:270
  13.8 0.0 copy-done.6
  13.8 0.0 copy-done.4
  13.8 0.0 copy-done.7
  13.8 0.0 copy-done.5
  13.9 9.8 %shard_map.113 = (f32[2,6,768,128]{3,2,1,0:T(8,128)S(1)}, f32[2,6,768,128]{3,2,1,0:T(8,128)S(1)}, f32[2,256,256]{2,1,0:T(8,128)S(1)}, f32[2,256,256]{2,1,0:T(8,128)S(1)}) custom-call(s32[1,1,32]{2,1,0:T(1,128)S(1)} %copy-done.2, s32[1,1,32]{2,1,0:T(1,128)S(1)} %copy-done.3, s32[1,1]{1,0:T(1,128)S(6)} %copy.38.count_ref, ...), custom_call_target="tpu_custom_call" | custom-call | flops 10000000000 | bytes 4000000 | tf_op jit(solution)/shard_map/pallas_call | solution.py:237
  23.7 0.0 collective-permute-done.4.refs_0_
  23.7 3.9 %shard_map.114 = (f32[2,6,768,128]{3,2,1,0:T(8,128)S(1)}, f32[2,6,768,128]{3,2,1,0:T(8,128)S(1)}, f32[2,256,256]{2,1,0:T(8,128)S(1)}, f32[2,256,256]{2,1,0:T(8,128)S(1)}) custom-call(s32[1,1,32]{2,1,0:T(1,128)S(1)} %copy-done.2, s32[1,1,32]{2,1,0:T(1,128)S(1)} %copy-done.3, ...), custom_call_target="tpu_custom_call", output_to_operand_aliasing={{0}: (9, {}), {1}: (10, {}), {2}: (11, {}), {3}: (12, {})} | custom-call | flops 10000000000 | bytes 4000000 | tf_op jit(solution)/shard_map/pallas_call | solution.py:237
  27.6 2.4 %collective-permute-done.3.refs_1_ = f32[2,128,256]{2,1,0:T(8,128)S(1)} collective-permute-done((f32[2,128,256]{2,1,0:T(8,128)S(1)}, f32[2,128,256]{2,1,0:T(8,128)S(1)}, u32[]{:S(2)}, u32[]{:S(2)}) %collective-permute-start.3) | collective-permute-done | bytes 262176 | tf_op jit(solution)/shard_map/ppermute | solution.py:270
  30.0 0.0 collective-permute-done.2.refs_0_
  30.0 5.8 %shard_map.115 = (f32[2,6,768,128]{3,2,1,0:T(8,128)S(1)}, f32[2,6,768,128]{3,2,1,0:T(8,128)S(1)}, f32[2,256,256]{2,1,0:T(8,128)S(1)}, f32[2,256,256]{2,1,0:T(8,128)S(1)}) custom-call(s32[1,1,32]{2,1,0:T(1,128)S(1)} %copy-done.2, s32[1,1,32]{2,1,0:T(1,128)S(1)} %copy-done.3, ...), custom_call_target="tpu_custom_call", output_to_operand_aliasing={{0}: (10, {}), {1}: (11, {}), {2}: (12, {}), {3}: (13, {})} | custom-call | flops 10000000000 | bytes 4000000 | tf_op jit(solution)/shard_map/pallas_call | solution.py:237
  35.8 10.6 %collective-permute-done.1.refs_1_ = f32[2,128,256]{2,1,0:T(8,128)S(1)} collective-permute-done((f32[2,128,256]{2,1,0:T(8,128)S(1)}, f32[2,128,256]{2,1,0:T(8,128)S(1)}, u32[]{:S(2)}, u32[]{:S(2)}) %collective-permute-start.1) | collective-permute-done | bytes 262176 | tf_op jit(solution)/shard_map/ppermute | solution.py:270
  46.4 0.0 collective-permute-done.refs_0_
  46.4 5.7 %shard_map.116 = (f32[2,6,768,128]{3,2,1,0:T(8,128)S(1)}, f32[2,6,768,128]{3,2,1,0:T(8,128)S(1)}, f32[2,256,256]{2,1,0:T(8,128)S(1)}, f32[2,256,256]{2,1,0:T(8,128)S(1)}) custom-call(s32[1,1,32]{2,1,0:T(1,128)S(1)} %copy-done.2, s32[1,1,32]{2,1,0:T(1,128)S(1)} %copy-done.3, ...), custom_call_target="tpu_custom_call", output_to_operand_aliasing={{0}: (10, {}), {1}: (11, {}), {2}: (12, {}), {3}: (13, {})} | custom-call | flops 10000000000 | bytes 4000000 | tf_op jit(solution)/shard_map/pallas_call | solution.py:237
  52.1 41.7 %shard_map.117 = (f32[2,512,512]{2,1,0:T(8,128)S(1)}, f32[2,256,256]{2,1,0:T(8,128)S(1)}) custom-call(f32[2,6,768,128]{3,2,1,0:T(8,128)S(1)} %get-tuple-element.28.upd_ref, f32[2,512,512]{2,1,0:T(8,128)S(1)} %copy-done, f32[512,256]{1,0:T(8,128)S(1)} %bitcast.1, f32[2,256,256]{2,1,0:T(8,128)S(1)} %copy-done.1), custom_call_target="tpu_custom_call" | custom-call | tf_op jit(solution)/shard_map/pallas_call | solution.py:420
  93.8 1.3 %copy.39 = f32[2,512,512]{2,1,0:T(8,128)} copy(f32[2,512,512]{2,1,0:T(8,128)S(1)} %get-tuple-element.36) | data formatting | bytes 4194304
  95.1 0.8 copy.40
  (4 shorter events, 0.0 us)
Async XLA Ops:
  0.6 13.2 %copy-start.6 = (bf16[2,256,256]{2,1,0:T(8,128)(2,1)S(1)}, bf16[2,256,256]{2,1,0:T(8,128)(2,1)}, u32[]{:S(2)}) copy-start(bf16[2,256,256]{2,1,0:T(8,128)(2,1)} %constant.10.clone.t3_ref) | copy-start | bytes 786436
  0.6 13.2 %copy-start.4 = (bf16[512,512]{1,0:T(8,128)(2,1)S(1)}, bf16[512,512]{1,0:T(8,128)(2,1)}, u32[]{:S(2)}) copy-start(bf16[512,512]{1,0:T(8,128)(2,1)} %constant.11.clone.t4_ref) | copy-start | bytes 1572868
  0.7 13.2 %copy-start.7 = (bf16[2,256,256]{2,1,0:T(8,128)(2,1)S(1)}, bf16[2,256,256]{2,1,0:T(8,128)(2,1)}, u32[]{:S(2)}) copy-start(bf16[2,256,256]{2,1,0:T(8,128)(2,1)} %constant.8.clone.t1_ref) | copy-start | bytes 786436
  0.7 13.2 %copy-start.5 = (bf16[512,512]{1,0:T(8,128)(2,1)S(1)}, bf16[512,512]{1,0:T(8,128)(2,1)}, u32[]{:S(2)}) copy-start(bf16[512,512]{1,0:T(8,128)(2,1)} %constant.9.clone.t2_ref) | copy-start | bytes 1572868
  0.7 13.2 %copy-start = (f32[2,512,512]{2,1,0:T(8,128)S(1)}, f32[2,512,512]{2,1,0:T(8,128)}, u32[]{:S(2)}) copy-start(f32[2,512,512]{2,1,0:T(8,128)} %obj_ref.1) | copy-start | bytes 6291460
  0.7 13.2 %copy-start.1 = (f32[2,256,256]{2,1,0:T(8,128)S(1)}, f32[2,256,256]{2,1,0:T(8,128)}, u32[]{:S(2)}) copy-start(f32[2,256,256]{2,1,0:T(8,128)} %probe_ref.1) | copy-start | bytes 1572868
  0.7 13.2 %copy-start.2 = (s32[1,1,32]{2,1,0:T(1,128)S(1)}, s32[1,1,32]{2,1,0:T(1,128)}, u32[]{:S(2)}) copy-start(s32[1,1,32]{2,1,0:T(1,128)} %rows_ref.7) | copy-start | bytes 388
  0.7 13.2 %copy-start.3 = (s32[1,1,32]{2,1,0:T(1,128)S(1)}, s32[1,1,32]{2,1,0:T(1,128)}, u32[]{:S(2)}) copy-start(s32[1,1,32]{2,1,0:T(1,128)} %cols_ref.7) | copy-start | bytes 388
  2.2 21.5 %collective-permute-start.4 = (f32[2,512,256]{2,1,0:T(8,128)S(1)}, f32[2,512,256]{2,1,0:T(8,128)S(1)}, u32[]{:S(2)}, u32[]{:S(2)}) collective-permute-start(f32[2,512,256]{2,1,0:T(8,128)S(1)} %slice.19), channel_id=1, source_target_pairs={{4,0},{8,4},{12,8},{16,12},{20,16},{24,20},{28,24},{32,28},{36,32}... | collective-permute-start | bytes 3145736 | tf_op jit(solution)/shard_map/ppermute | solution.py:264
  6.9 23.1 %collective-permute-start.2 = (f32[2,128,512]{2,1,0:T(8,128)S(1)}, f32[2,128,512]{2,1,0:T(8,128)S(1)}, u32[]{:S(2)}, u32[]{:S(2)}) collective-permute-start(f32[2,128,512]{2,1,0:T(8,128)S(1)} %get-tuple-element.32), channel_id=1, source_target_pairs={{1,0},{2,1},{3,2},{5,4},{6,5},{7,6},{9,8},{10,9},{11,10},{13,12},{... | collective-permute-start | bytes 1572872 | tf_op jit(solution)/shard_map/ppermute | solution.py:264
  9.3 20.7 %collective-permute-start.3 = (f32[2,128,256]{2,1,0:T(8,128)S(1)}, f32[2,128,256]{2,1,0:T(8,128)S(1)}, u32[]{:S(2)}, u32[]{:S(2)}) collective-permute-start(f32[2,128,256]{2,1,0:T(8,128)S(1)} %get-tuple-element.30), channel_id=1, source_target_pairs={{5,0},{6,1},{7,2},{9,4},{10,5},{11,6},{13,8},{14,9},{15,10},{17,12... | collective-permute-start | bytes 786440 | tf_op jit(solution)/shard_map/ppermute | solution.py:270
  10.6 35.8 %collective-permute-start = (f32[2,128,512]{2,1,0:T(8,128)S(1)}, f32[2,128,512]{2,1,0:T(8,128)S(1)}, u32[]{:S(2)}, u32[]{:S(2)}) collective-permute-start(f32[2,128,512]{2,1,0:T(8,128)S(1)} %get-tuple-element.33), channel_id=1, source_target_pairs={{1,0},{2,1},{3,2},{5,4},{6,5},{7,6},{9,8},{10,9},{11,10},{13,12},{... | collective-permute-start | bytes 1572872 | tf_op jit(solution)/shard_map/ppermute | solution.py:264
  11.9 34.5 %collective-permute-start.1 = (f32[2,128,256]{2,1,0:T(8,128)S(1)}, f32[2,128,256]{2,1,0:T(8,128)S(1)}, u32[]{:S(2)}, u32[]{:S(2)}) collective-permute-start(f32[2,128,256]{2,1,0:T(8,128)S(1)} %get-tuple-element.31), channel_id=1, source_target_pairs={{5,0},{6,1},{7,2},{9,4},{10,5},{11,6},{13,8},{14,9},{15,10},{17,12... | collective-permute-start | bytes 786440 | tf_op jit(solution)/shard_map/ppermute | solution.py:270

commit v5 on v4

--- a/solution.py
+++ b/solution.py
@@ -38,8 +38,14 @@
     return np.stack(first), second, np.stack(third), fourth
 
 
+def slot_class(r, c):
+    reach = BLOCK - N
+    lower = 2 + (r > reach + H).astype(jnp.int32)
+    return jnp.where(r > reach, lower, (c > reach).astype(jnp.int32))
+
+
 def slots_kernel(
-    rule, places, first, last,
+    stage, places, first, last,
     rows_ref, cols_ref, count_ref, amp_ref, t1_ref, t2_ref, t3_ref, t4_ref, *refs,
 ):
     n_pieces = len(places)
@@ -62,15 +68,31 @@
         for b in range(w // H):
             bring(piece.at[:, :, b * H : (b + 1) * H], ext.at[:, c0 // H + b, r0 : r0 + h, :])
 
-    def collect(s, n):
-        order[n] = s
-        keep = jnp.logical_and(s < count_ref[0, 0], rule(rows_ref[0, 0, s], cols_ref[0, 0, s]))
-        return n + keep.astype(jnp.int32)
-
-    total = lax.fori_loop(0, rows_ref.shape[2], collect, jnp.int32(0))
+    def collect(s, carry):
+        n, before, best, pick = carry
+        live = s < count_ref[0, 0]
+        level = slot_class(rows_ref[0, 0, s], cols_ref[0, 0, s])
+        earlier = jnp.logical_and(live, level < stage)
+        newer = jnp.logical_and(earlier, level >= best)
+        order[n + 1] = s
+        return (
+            n + jnp.logical_and(live, level == stage).astype(jnp.int32),
+            before + earlier.astype(jnp.int32),
+            jnp.where(newer, level, best),
+            jnp.where(newer, s, pick),
+        )
+
+    zero = jnp.int32(0)
+    total, before, _, pick = lax.fori_loop(0, rows_ref.shape[2], collect, (zero, zero, zero, zero))
+    waiting = lax.rem(before, 2)
+    order[0] = pick
+    base = 1 - waiting
+    total = total + waiting
+    if not last:
+        total = total - lax.rem(total, 2)
 
     def amp_copy(i, k=0):
-        return pltpu.make_async_copy(amp_ref.at[0, 0, order[i]], amp_buf[k], amp_sem.at[k])
+        return pltpu.make_async_copy(amp_ref.at[0, 0, order[base + i]], amp_buf[k], amp_sem.at[k])
 
     final = jnp.maximum(total - 1, 0)
     pairs = (total + 1) // 2
@@ -101,7 +123,7 @@
     dot = functools.partial(jnp.dot, preferred_element_type=jnp.float32)
 
     def place(i):
-        s = order[i]
+        s = order[base + i]
         c = cols_ref[0, 0, s]
         return rows_ref[0, 0, s], c // H, lax.rem(c, H)
 
@@ -226,7 +248,7 @@
                 psum_ref[comp, :, lanes] = lanes_buf[comp, b]
 
 
-def run_slots(rule, places, pieces, state, last, scalars, amplitudes, tables):
+def run_slots(stage, places, pieces, state, last, scalars, amplitudes, tables):
     smem = pl.BlockSpec(memory_space=pltpu.SMEM)
     vmem = pl.BlockSpec(memory_space=pltpu.VMEM)
     hbm = pl.BlockSpec(memory_space=pl.ANY)
@@ -235,7 +257,7 @@
     shapes = [(2, WIDE // H, WIDE, H)] * 2 + [(2, N, N)] * 2
     at = 8 + len(pieces)
     return pl.pallas_call(
-        functools.partial(slots_kernel, rule, places, first, last),
+        functools.partial(slots_kernel, stage, places, first, last),
         out_shape=tuple(jax.ShapeDtypeStruct(shape, jnp.float32) for shape in shapes),
         in_specs=[smem] * 3 + [far] + [vmem] * 4 + [hbm] * len(pieces) + ([hbm] if first else [vmem] * 4),
         out_specs=(vmem,) * 4,
@@ -455,14 +477,11 @@
         corners.append(from_diagonal(object_field[:, rows, :N]))
     right = passed_along(object_field[:, :, :N], "pos", -1)
     fixed = ((corner_rows, corner_cols, counts), amplitudes, tables)
-    reach = BLOCK - N
-    state = run_slots(
-        lambda r, c: (r <= reach) & (c <= reach), ((0, 0),), (object_field,), (probe,), False, *fixed
-    )
-    state = run_slots(lambda r, c: (r <= reach) & (c > reach), ((0, BLOCK),), (right,), state, False, *fixed)
-    for q, rule in enumerate((lambda r, c: (r > reach) & (r <= reach + H), lambda r, c: r > reach + H)):
+    state = run_slots(0, ((0, 0),), (object_field,), (probe,), False, *fixed)
+    state = run_slots(1, ((0, BLOCK),), (right,), state, False, *fixed)
+    for q in range(2):
         row = BLOCK + q * H
-        state = run_slots(rule, ((row, 0), (row, BLOCK)), (lows[q], corners[q]), state, q == 1, *fixed)
+        state = run_slots(2 + q, ((row, 0), (row, BLOCK)), (lows[q], corners[q]), state, q == 1, *fixed)
     _, update, total, _ = state
     return exchange(update, object_field, total.reshape(2 * N, N), probe)
 

time: 96.8 us -> 95.6 us (0.988); the launches traced: 95.9 us -> 95.7 us
  Pallas kernels: 66.9 us -> 65.2 us
  waiting for transfers between devices: 13 us -> 14.5 us
    ppermute x2, waiting for transfers between devices: 12.9 us -> 14.3 us  [from_diagonal(): return lax.ppermute(block, ('pos', 'tile'), route)]
    pallas_call x4, Pallas kernels: 25.2 us -> 24.1 us  [run_slots(): pl.pallas_call(functools.partial(slots_kernel, stage, places, first, last...]
  transfers between devices with their start and end apart: 5 -> 5, of which waited for: 2 -> 3; matrix products, arithmetic and copies ran while one was open for 2% -> 2% of each run, Pallas kernels for 20% -> 19%
where the time goes in v5:
time: 95.6 us; the launch traced here: 95.7 us
  Pallas kernels  65.2 us (68%)
  waiting for transfers between devices  14.5 us (15%)
  starting transfers between devices  8.59 us (9%)
  local copies, waits for them, and re-layouts  5.96 us (6%)
  between operations  1.5 us (2%)
    pallas_call x1, Pallas kernels, exchange(): pl.pallas_call(exchange_kernel, out_shape=(jax.ShapeDtypeStruct((2, BLOCK...  41 us
    pallas_call x4, Pallas kernels, run_slots(): pl.pallas_call(functools.partial(slots_kernel, stage, places, first, last...  24.1 us
    ppermute x2, waiting for transfers between devices, from_diagonal(): return lax.ppermute(block, ('pos', 'tile'), route)  14.3 us
    ppermute x3, starting transfers between devices, passed_along(): return lax.ppermute(block, axis, route)  6.01 us
    ppermute x2, starting transfers between devices, from_diagonal(): return lax.ppermute(block, ('pos', 'tile'), route)  2.58 us
    unnamed x18, local copies, waits for them, and re-layouts  2.16 us
  transfers between devices with their start and end apart: 5, of which 3 were waited for; matrix products, arithmetic and copies ran while one was open for 2% of the time, Pallas kernels for 19%

profile of v5, /device:TPU:1, one launch (start us, length us, event | category | flops | bytes accessed | tf_op | source)
XLA Modules:
  0.0 95.7 jit_solution(2544249777460210124)
XLA Ops:
  0.6 0.0 copy-start.6
  0.6 0.0 copy-start.4
  0.7 0.0 copy-start.7
  0.7 0.0 copy-start.5
  0.7 0.0 copy-start
  0.7 0.0 copy-start.1
  0.7 0.0 copy-start.2
  0.7 0.0 copy-start.3
  0.7 1.4 %slice.19 = f32[2,512,256]{2,1,0:T(8,128)S(1)} slice(f32[2,512,512]{2,1,0:T(8,128)} %obj_ref.1), slice={[0:2], [0:512], [0:256]} | slice | bytes 2097152 | tf_op jit(solution)/shard_map/slice | solution.py:478
  2.2 3.4 %collective-permute-start.4 = (f32[2,512,256]{2,1,0:T(8,128)S(1)}, f32[2,512,256]{2,1,0:T(8,128)S(1)}, u32[]{:S(2)}, u32[]{:S(2)}) collective-permute-start(f32[2,512,256]{2,1,0:T(8,128)S(1)} %slice.19), channel_id=1, source_target_pairs={{4,0},{8,4},{12,8},{16,12},{20,16},{24,20},{28,24},{32,28},{36,32}... | collective-permute-start | bytes 3145736 | tf_op jit(solution)/shard_map/ppermute | solution.py:286
  5.6 1.3 %fusion.1 = (f32[2,128,512]{2,1,0:T(8,128)S(1)}, f32[2,128,512]{2,1,0:T(8,128)S(1)}) fusion(f32[2,512,512]{2,1,0:T(8,128)} %obj_ref.1), kind=kLoop, calls=%fused_computation.1 | loop fusion | bytes 2097152 | tf_op jit(solution)/shard_map/slice | solution.py:476
  6.9 1.3 %collective-permute-start.2 = (f32[2,128,512]{2,1,0:T(8,128)S(1)}, f32[2,128,512]{2,1,0:T(8,128)S(1)}, u32[]{:S(2)}, u32[]{:S(2)}) collective-permute-start(f32[2,128,512]{2,1,0:T(8,128)S(1)} %get-tuple-element.32), channel_id=1, source_target_pairs={{1,0},{2,1},{3,2},{5,4},{6,5},{7,6},{9,8},{10,9},{11,10},{13,12},{... | collective-permute-start | bytes 1572872 | tf_op jit(solution)/shard_map/ppermute | solution.py:286
  8.2 1.1 %fusion = (f32[2,128,256]{2,1,0:T(8,128)S(1)}, f32[2,128,256]{2,1,0:T(8,128)S(1)}) fusion(f32[2,512,512]{2,1,0:T(8,128)} %obj_ref.1), kind=kLoop, calls=%fused_computation | loop fusion | bytes 1048576 | tf_op jit(solution)/shard_map/slice | solution.py:477
  9.3 1.3 %collective-permute-start.3 = (f32[2,128,256]{2,1,0:T(8,128)S(1)}, f32[2,128,256]{2,1,0:T(8,128)S(1)}, u32[]{:S(2)}, u32[]{:S(2)}) collective-permute-start(f32[2,128,256]{2,1,0:T(8,128)S(1)} %get-tuple-element.30), channel_id=1, source_target_pairs={{5,0},{6,1},{7,2},{9,4},{10,5},{11,6},{13,8},{14,9},{15,10},{17,12... | collective-permute-start | bytes 786440 | tf_op jit(solution)/shard_map/ppermute | solution.py:292
  10.6 1.3 %collective-permute-start = (f32[2,128,512]{2,1,0:T(8,128)S(1)}, f32[2,128,512]{2,1,0:T(8,128)S(1)}, u32[]{:S(2)}, u32[]{:S(2)}) collective-permute-start(f32[2,128,512]{2,1,0:T(8,128)S(1)} %get-tuple-element.33), channel_id=1, source_target_pairs={{1,0},{2,1},{3,2},{5,4},{6,5},{7,6},{9,8},{10,9},{11,10},{13,12},{... | collective-permute-start | bytes 1572872 | tf_op jit(solution)/shard_map/ppermute | solution.py:286
  11.9 1.3 %collective-permute-start.1 = (f32[2,128,256]{2,1,0:T(8,128)S(1)}, f32[2,128,256]{2,1,0:T(8,128)S(1)}, u32[]{:S(2)}, u32[]{:S(2)}) collective-permute-start(f32[2,128,256]{2,1,0:T(8,128)S(1)} %get-tuple-element.31), channel_id=1, source_target_pairs={{5,0},{6,1},{7,2},{9,4},{10,5},{11,6},{13,8},{14,9},{15,10},{17,12... | collective-permute-start | bytes 786440 | tf_op jit(solution)/shard_map/ppermute | solution.py:292
  13.8 0.0 copy-done.6
  13.8 0.0 copy-done.4
  13.8 0.0 copy-done.7
  13.8 0.0 copy-done.5
  13.9 6.0 %shard_map.113 = (f32[2,6,768,128]{3,2,1,0:T(8,128)S(1)}, f32[2,6,768,128]{3,2,1,0:T(8,128)S(1)}, f32[2,256,256]{2,1,0:T(8,128)S(1)}, f32[2,256,256]{2,1,0:T(8,128)S(1)}) custom-call(s32[1,1,32]{2,1,0:T(1,128)S(1)} %copy-done.2, s32[1,1,32]{2,1,0:T(1,128)S(1)} %copy-done.3, s32[1,1]{1,0:T(1,128)S(6)} %copy.38.count_ref, ...), custom_call_target="tpu_custom_call" | custom-call | flops 10000000000 | bytes 4000000 | tf_op jit(solution)/shard_map/pallas_call | solution.py:259
  19.9 0.1 collective-permute-done.4.refs_0_
  20.0 6.0 %shard_map.114 = (f32[2,6,768,128]{3,2,1,0:T(8,128)S(1)}, f32[2,6,768,128]{3,2,1,0:T(8,128)S(1)}, f32[2,256,256]{2,1,0:T(8,128)S(1)}, f32[2,256,256]{2,1,0:T(8,128)S(1)}) custom-call(s32[1,1,32]{2,1,0:T(1,128)S(1)} %copy-done.2, s32[1,1,32]{2,1,0:T(1,128)S(1)} %copy-done.3, ...), custom_call_target="tpu_custom_call", output_to_operand_aliasing={{0}: (9, {}), {1}: (10, {}), {2}: (11, {}), {3}: (12, {})} | custom-call | flops 10000000000 | bytes 4000000 | tf_op jit(solution)/shard_map/pallas_call | solution.py:259
  26.0 4.0 %collective-permute-done.3.refs_1_ = f32[2,128,256]{2,1,0:T(8,128)S(1)} collective-permute-done((f32[2,128,256]{2,1,0:T(8,128)S(1)}, f32[2,128,256]{2,1,0:T(8,128)S(1)}, u32[]{:S(2)}, u32[]{:S(2)}) %collective-permute-start.3) | collective-permute-done | bytes 262176 | tf_op jit(solution)/shard_map/ppermute | solution.py:292
  30.0 0.0 collective-permute-done.2.refs_0_
  30.0 6.0 %shard_map.115 = (f32[2,6,768,128]{3,2,1,0:T(8,128)S(1)}, f32[2,6,768,128]{3,2,1,0:T(8,128)S(1)}, f32[2,256,256]{2,1,0:T(8,128)S(1)}, f32[2,256,256]{2,1,0:T(8,128)S(1)}) custom-call(s32[1,1,32]{2,1,0:T(1,128)S(1)} %copy-done.2, s32[1,1,32]{2,1,0:T(1,128)S(1)} %copy-done.3, ...), custom_call_target="tpu_custom_call", output_to_operand_aliasing={{0}: (10, {}), {1}: (11, {}), {2}: (12, {}), {3}: (13, {})} | custom-call | flops 10000000000 | bytes 4000000 | tf_op jit(solution)/shard_map/pallas_call | solution.py:259
  36.0 10.3 %collective-permute-done.1.refs_1_ = f32[2,128,256]{2,1,0:T(8,128)S(1)} collective-permute-done((f32[2,128,256]{2,1,0:T(8,128)S(1)}, f32[2,128,256]{2,1,0:T(8,128)S(1)}, u32[]{:S(2)}, u32[]{:S(2)}) %collective-permute-start.1) | collective-permute-done | bytes 262176 | tf_op jit(solution)/shard_map/ppermute | solution.py:292
  46.4 0.0 collective-permute-done.refs_0_
  46.4 6.1 %shard_map.116 = (f32[2,6,768,128]{3,2,1,0:T(8,128)S(1)}, f32[2,6,768,128]{3,2,1,0:T(8,128)S(1)}, f32[2,256,256]{2,1,0:T(8,128)S(1)}, f32[2,256,256]{2,1,0:T(8,128)S(1)}) custom-call(s32[1,1,32]{2,1,0:T(1,128)S(1)} %copy-done.2, s32[1,1,32]{2,1,0:T(1,128)S(1)} %copy-done.3, ...), custom_call_target="tpu_custom_call", output_to_operand_aliasing={{0}: (10, {}), {1}: (11, {}), {2}: (12, {}), {3}: (13, {})} | custom-call | flops 10000000000 | bytes 4000000 | tf_op jit(solution)/shard_map/pallas_call | solution.py:259
  52.5 41.0 %shard_map.117 = (f32[2,512,512]{2,1,0:T(8,128)S(1)}, f32[2,256,256]{2,1,0:T(8,128)S(1)}) custom-call(f32[2,6,768,128]{3,2,1,0:T(8,128)S(1)} %get-tuple-element.28.upd_ref, f32[2,512,512]{2,1,0:T(8,128)S(1)} %copy-done, f32[512,256]{1,0:T(8,128)S(1)} %bitcast.1, f32[2,256,256]{2,1,0:T(8,128)S(1)} %copy-done.1), custom_call_target="tpu_custom_call" | custom-call | tf_op jit(solution)/shard_map/pallas_call | solution.py:442
  93.6 1.3 %copy.39 = f32[2,512,512]{2,1,0:T(8,128)} copy(f32[2,512,512]{2,1,0:T(8,128)S(1)} %get-tuple-element.36) | data formatting | bytes 4194304
  94.9 0.8 copy.40
  (4 shorter events, 0.0 us)
Async XLA Ops:
  0.6 13.2 %copy-start.6 = (bf16[2,256,256]{2,1,0:T(8,128)(2,1)S(1)}, bf16[2,256,256]{2,1,0:T(8,128)(2,1)}, u32[]{:S(2)}) copy-start(bf16[2,256,256]{2,1,0:T(8,128)(2,1)} %constant.10.clone.t3_ref) | copy-start | bytes 786436
  0.6 13.2 %copy-start.4 = (bf16[512,512]{1,0:T(8,128)(2,1)S(1)}, bf16[512,512]{1,0:T(8,128)(2,1)}, u32[]{:S(2)}) copy-start(bf16[512,512]{1,0:T(8,128)(2,1)} %constant.11.clone.t4_ref) | copy-start | bytes 1572868
  0.7 13.2 %copy-start.7 = (bf16[2,256,256]{2,1,0:T(8,128)(2,1)S(1)}, bf16[2,256,256]{2,1,0:T(8,128)(2,1)}, u32[]{:S(2)}) copy-start(bf16[2,256,256]{2,1,0:T(8,128)(2,1)} %constant.8.clone.t1_ref) | copy-start | bytes 786436
  0.7 13.2 %copy-start.5 = (bf16[512,512]{1,0:T(8,128)(2,1)S(1)}, bf16[512,512]{1,0:T(8,128)(2,1)}, u32[]{:S(2)}) copy-start(bf16[512,512]{1,0:T(8,128)(2,1)} %constant.9.clone.t2_ref) | copy-start | bytes 1572868
  0.7 13.2 %copy-start = (f32[2,512,512]{2,1,0:T(8,128)S(1)}, f32[2,512,512]{2,1,0:T(8,128)}, u32[]{:S(2)}) copy-start(f32[2,512,512]{2,1,0:T(8,128)} %obj_ref.1) | copy-start | bytes 6291460
  0.7 13.2 %copy-start.1 = (f32[2,256,256]{2,1,0:T(8,128)S(1)}, f32[2,256,256]{2,1,0:T(8,128)}, u32[]{:S(2)}) copy-start(f32[2,256,256]{2,1,0:T(8,128)} %probe_ref.1) | copy-start | bytes 1572868
  0.7 13.2 %copy-start.2 = (s32[1,1,32]{2,1,0:T(1,128)S(1)}, s32[1,1,32]{2,1,0:T(1,128)}, u32[]{:S(2)}) copy-start(s32[1,1,32]{2,1,0:T(1,128)} %rows_ref.7) | copy-start | bytes 388
  0.7 13.2 %copy-start.3 = (s32[1,1,32]{2,1,0:T(1,128)S(1)}, s32[1,1,32]{2,1,0:T(1,128)}, u32[]{:S(2)}) copy-start(s32[1,1,32]{2,1,0:T(1,128)} %cols_ref.7) | copy-start | bytes 388
  2.2 17.8 %collective-permute-start.4 = (f32[2,512,256]{2,1,0:T(8,128)S(1)}, f32[2,512,256]{2,1,0:T(8,128)S(1)}, u32[]{:S(2)}, u32[]{:S(2)}) collective-permute-start(f32[2,512,256]{2,1,0:T(8,128)S(1)} %slice.19), channel_id=1, source_target_pairs={{4,0},{8,4},{12,8},{16,12},{20,16},{24,20},{28,24},{32,28},{36,32}... | collective-permute-start | bytes 3145736 | tf_op jit(solution)/shard_map/ppermute | solution.py:286
  6.9 23.1 %collective-permute-start.2 = (f32[2,128,512]{2,1,0:T(8,128)S(1)}, f32[2,128,512]{2,1,0:T(8,128)S(1)}, u32[]{:S(2)}, u32[]{:S(2)}) collective-permute-start(f32[2,128,512]{2,1,0:T(8,128)S(1)} %get-tuple-element.32), channel_id=1, source_target_pairs={{1,0},{2,1},{3,2},{5,4},{6,5},{7,6},{9,8},{10,9},{11,10},{13,12},{... | collective-permute-start | bytes 1572872 | tf_op jit(solution)/shard_map/ppermute | solution.py:286
  9.3 20.7 %collective-permute-start.3 = (f32[2,128,256]{2,1,0:T(8,128)S(1)}, f32[2,128,256]{2,1,0:T(8,128)S(1)}, u32[]{:S(2)}, u32[]{:S(2)}) collective-permute-start(f32[2,128,256]{2,1,0:T(8,128)S(1)} %get-tuple-element.30), channel_id=1, source_target_pairs={{5,0},{6,1},{7,2},{9,4},{10,5},{11,6},{13,8},{14,9},{15,10},{17,12... | collective-permute-start | bytes 786440 | tf_op jit(solution)/shard_map/ppermute | solution.py:292
  10.6 35.8 %collective-permute-start = (f32[2,128,512]{2,1,0:T(8,128)S(1)}, f32[2,128,512]{2,1,0:T(8,128)S(1)}, u32[]{:S(2)}, u32[]{:S(2)}) collective-permute-start(f32[2,128,512]{2,1,0:T(8,128)S(1)} %get-tuple-element.33), channel_id=1, source_target_pairs={{1,0},{2,1},{3,2},{5,4},{6,5},{7,6},{9,8},{10,9},{11,10},{13,12},{... | collective-permute-start | bytes 1572872 | tf_op jit(solution)/shard_map/ppermute | solution.py:286
  11.9 34.5 %collective-permute-start.1 = (f32[2,128,256]{2,1,0:T(8,128)S(1)}, f32[2,128,256]{2,1,0:T(8,128)S(1)}, u32[]{:S(2)}, u32[]{:S(2)}) collective-permute-start(f32[2,128,256]{2,1,0:T(8,128)S(1)} %get-tuple-element.31), channel_id=1, source_target_pairs={{5,0},{6,1},{7,2},{9,4},{10,5},{11,6},{13,8},{14,9},{15,10},{17,12... | collective-permute-start | bytes 786440 | tf_op jit(solution)/shard_map/ppermute | solution.py:292
